TPU v7x, 768 devices: a whole 4x8x12 slice. The times are simulated.
768 devices in a mesh: dp: 64 (over y, z_hi, x), fsdp: 12 (over z_lo, core).
Axes of the slice: x: 4, y: 8, z: 12 (z_hi: 2, z_lo: 6; z = z_hi * 6 + z_lo), core: 2. Of those that a mesh axis runs over, the one named last changes fastest.
Arguments:
- z_a: bfloat16 [12288, 4224], P('dp', 'fsdp'), may hold values from -200 to 200
- z_b: bfloat16 [12288, 4224], P('dp'), may hold values from -200 to 200
Outputs:
- grad_a: bfloat16 [12288, 4224], P('dp', 'fsdp')
- grad_b: bfloat16 [12288, 4224], P('dp', 'fsdp')
All inputs are finite; a program needn't handle non-finite values.
Results may differ from a plain program's by a relative error of at most 0.02.
Values may be sent and summed in bfloat16 or wider, within the bound.
A program may use at most 64 MiB of HBM per device.

v0:
```python
import jax
import jax.numpy as jnp
from jax import lax
from jax.sharding import PartitionSpec as P

eps = 1e-05
offdiag_weight = 0.0051


def scaled(values, total, squares, batch):
    center = total / batch
    inverse = lax.rsqrt(squares / batch - center * center + eps)
    return ((values - center) * inverse, inverse)


def grad_block(owned, first_col, offset, block):
    span = owned.shape[0]
    col_ids = first_col + jnp.arange(span, dtype=jnp.int32)[:, None]
    row_ids = offset + jnp.arange(block, dtype=jnp.int32)[None, :]
    return jnp.where(col_ids == row_ids, -2.0 * (1.0 - owned), 2.0 * offdiag_weight * owned).astype(
        jnp.bfloat16
    )


def local(z_a, z_b):
    rows, block = z_a.shape
    groups = lax.axis_size("dp")
    batch = rows * groups
    first = z_a.astype(jnp.float32)
    second = z_b.astype(jnp.float32)
    moments = lax.psum(
        (
            jnp.sum(first, axis=0),
            jnp.sum(first * first, axis=0),
            jnp.sum(second, axis=0),
            jnp.sum(second * second, axis=0),
        ),
        "dp",
    )
    norm_a, inv_a = scaled(first, moments[0], moments[1], batch)
    norm_b, inv_b = scaled(second, moments[2], moments[3], batch)
    low_a = norm_a.astype(jnp.bfloat16)
    low_b = norm_b.astype(jnp.bfloat16)
    offset = lax.axis_index("fsdp") * block
    piece = low_b
    owned = (
        lax.psum_scatter(
            lax.dot_general(
                piece, low_a, (((0,), (0,)), ((), ())), preferred_element_type=jnp.float32
            ),
            "dp",
            scatter_dimension=0,
            tiled=True,
        )
        / batch
    )
    grad_t = grad_block(owned, lax.axis_index("dp") * owned.shape[0], offset, block)
    piece = lax.all_gather(grad_t, "dp", axis=0, tiled=True)
    total_a = jnp.dot(low_b, piece, preferred_element_type=jnp.float32)
    part_cols = lax.dot_general(
        low_a, piece, (((1,), (1,)), ((), ())), preferred_element_type=jnp.float32
    )
    norm_own = lax.dynamic_slice_in_dim(norm_b, offset, block, 1)
    inv_own = lax.dynamic_slice_in_dim(inv_b, offset, block, 0)
    back_b = lax.psum_scatter(
        part_cols.astype(jnp.bfloat16), "fsdp", scatter_dimension=1, tiled=True
    ).astype(jnp.float32)
    sums_a = lax.psum((jnp.sum(total_a, axis=0), jnp.sum(total_a * norm_a, axis=0)), "dp")
    sums_b = lax.psum((jnp.sum(back_b, axis=0), jnp.sum(back_b * norm_own, axis=0)), "dp")
    grad_a = inv_a * (total_a - sums_a[0] / batch - norm_a * (sums_a[1] / batch))
    grad_b = inv_own * (back_b - sums_b[0] / batch - norm_own * (sums_b[1] / batch))
    return (grad_a.astype(jnp.bfloat16), grad_b.astype(jnp.bfloat16))


def solution(mesh):
    return jax.shard_map(
        local,
        mesh=mesh,
        in_specs=(P("dp", "fsdp"), P("dp", None)),
        out_specs=(P("dp", "fsdp"), P("dp", "fsdp")),
        check_vma=False,
    )
```

profile of v0, /device:TPU:1, one launch (start us, length us, event | category | flops | bytes accessed | tf_op | source)
XLA Modules:
  0.0 1444.5 jit_solution(7585527422091411466)
XLA Ops:
  7.2 2.0 convert_reduce_fusion
  9.2 1.0 fusion.9
  10.2 468.4 %all-reduce.3 = (f32[4224]{0:T(1024)S(1)}, f32[4224]{0:T(1024)S(1)}, f32[352]{0:T(512)S(1)}, f32[352]{0:T(512)S(1)}) all-reduce(f32[4224]{0:T(1024)S(1)} %get-tuple-element.3, f32[4224]{0:T(1024)S(1)} %get-tuple-element.2, f32[352]{0:T(512)S(1)} %get-tuple-element.9, ...), channel_id=1, replica_groups=mesh['dp'=64,'fsdp'=12] {'dp'}, use_global_device_ids=true, to_apply=%region_7.0 | all-reduce | flops 9152 | bytes 73216 | tf_op jit(solution)/shard_map/psum | solution.py:31
  479.2 5.0 fusion.5
  484.2 322.3 %fusion = f32[80,352]{1,0:T(8,128)S(1)} fusion(f32[4224,352]{1,0:T(8,128)} %fusion.5), kind=kCustom, calls=%all-reduce-scatter | all-reduce-scatter fusion | flops 1802241 | bytes 6064128
  806.5 1.3 collective-permute-start.10
  807.8 1.3 collective-permute-start.11
  809.1 3.9 collective-permute-start.9
  813.0 1.3 collective-permute-start.8
  814.3 1.3 collective-permute-start.7
  815.6 1.3 collective-permute-start.6
  816.9 17.5 %collective-permute-start.5 = (f32[80,352]{1,0:T(8,128)S(1)}, f32[80,352]{1,0:T(8,128)S(1)}, u32[]{:S(2)}, u32[]{:S(2)}) collective-permute-start(f32[80,352]{1,0:T(8,128)S(1)} %fusion), channel_id=1, source_target_pairs={{0,72},{12,84},{24,96},{36,108},{48,120},{60,132},{72,144},{84,156... | collective-permute-start | bytes 337928
  834.5 1.3 dynamic-slice.4
  835.8 1.3 collective-permute-start.4
  837.1 9.4 collective-permute-start.3
  846.6 1.3 collective-permute-start.2
  847.9 5.5 collective-permute-start.1
  853.5 2.5 collective-permute-start
  858.0 9.3 concatenate
  868.2 247.5 %all-gather.3.cloned.1.call-done = bf16[64,66,352]{2,1,0:T(8,128)(2,1)} async-done(((bf16[1,66,352]{2,1,0:T(8,128)(2,1)}), bf16[64,66,352]{2,1,0:T(8,128)(2,1)}) %all-gather.3.cloned.1.call-update) | async-done | bytes 2973712 | tf_op jit(solution)/shard_map/all_gather | solution.py:58
  1115.7 5.8 reshape.24
  1121.6 3.2 convolution_convert_fusion
  1124.8 2.5 copy.4
  1127.4 2.0 fusion.1
  1129.5 1.0 copy-done.1
  1130.4 1.1 fusion.25
  1131.5 62.6 %reduce-scatter.6.cloned.1.call-done = bf16[352,192]{1,0:T(8,128)(2,1)} async-done(((bf16[4224,192]{1,0:T(8,128)(2,1)}), bf16[352,192]{1,0:T(8,128)(2,1)}) %reduce-scatter.6.cloned.1.call-update) | async-done | bytes 135184
  1194.1 1.1 copy.5
  1195.2 1.2 convert_reduce_fusion.1
  1196.4 238.8 %all-reduce.2 = (f32[352]{0:T(512)S(1)}, f32[352]{0:T(512)S(1)}, f32[352]{0:T(512)S(1)}, f32[352]{0:T(512)S(1)}) all-reduce(f32[352]{0:T(512)S(1)} %get-tuple-element.5, f32[352]{0:T(512)S(1)} %get-tuple-element.4, f32[352]{0:T(512)S(1)} %get-tuple-element.7, f32[352]{0:T(512)S(1)} %get-tuple-element.6), channel_id=1, replica_groups=mesh['dp'=64,'fsdp'=12] {'dp'}, use_global_device_ids=true, to_apply=%region_12.13 | all-reduce | flops 1408 | bytes 11264 | tf_op jit(solution)/shard_map/psum | solution.py:68
  1435.1 0.7 fusion.17
  1435.9 1.8 fusion.20
  (54 shorter events, 2.9 us)
Async XLA Ops:
  7.2 472.0 %copy-start = (bf16[192,4224]{1,0:T(8,128)(2,1)S(1)}, bf16[192,4224]{1,0:T(8,128)(2,1)}, u32[]{:S(2)}) copy-start(bf16[192,4224]{1,0:T(8,128)(2,1)} %param.3) | copy-start | bytes 4866052
  7.2 1108.5 %all-gather.3.cloned.1.call-start = ((), (), s32[]{:S(2)}) async-start(), calls=%async_computation.1 | async-start | bytes 3594240 | tf_op jit(solution)/shard_map/all_gather | solution.py:58
  478.6 0.6 copy-start.11
  478.6 0.6 copy-start.13
  806.5 10.4 collective-permute-start.10
  807.8 7.8 collective-permute-start.11
  809.1 26.7 %collective-permute-start.9 = (f32[80,352]{1,0:T(8,128)S(1)}, f32[80,352]{1,0:T(8,128)S(1)}, u32[]{:S(2)}, u32[]{:S(2)}) collective-permute-start(f32[80,352]{1,0:T(8,128)S(1)} %fusion), channel_id=1, source_target_pairs={{0,120},{12,132},{24,144},{36,156},{48,168},{60,180},{72,192},{84,... | collective-permute-start | bytes 337928
  813.0 24.1 %collective-permute-start.8 = (f32[80,352]{1,0:T(8,128)S(1)}, f32[80,352]{1,0:T(8,128)S(1)}, u32[]{:S(2)}, u32[]{:S(2)}) collective-permute-start(f32[80,352]{1,0:T(8,128)S(1)} %fusion), channel_id=1, source_target_pairs={{0,108},{12,120},{24,132},{36,144},{48,156},{60,168},{72,180},{84,... | collective-permute-start | bytes 337928
  814.3 32.2 %collective-permute-start.7 = (f32[80,352]{1,0:T(8,128)S(1)}, f32[80,352]{1,0:T(8,128)S(1)}, u32[]{:S(2)}, u32[]{:S(2)}) collective-permute-start(f32[80,352]{1,0:T(8,128)S(1)} %fusion), channel_id=1, source_target_pairs={{0,96},{12,108},{24,120},{36,132},{48,144},{60,156},{72,168},{84,1... | collective-permute-start | bytes 337928
  815.6 32.2 %collective-permute-start.6 = (f32[80,352]{1,0:T(8,128)S(1)}, f32[80,352]{1,0:T(8,128)S(1)}, u32[]{:S(2)}, u32[]{:S(2)}) collective-permute-start(f32[80,352]{1,0:T(8,128)S(1)} %fusion), channel_id=1, source_target_pairs={{0,84},{12,96},{24,108},{36,120},{48,132},{60,144},{72,156},{84,16... | collective-permute-start | bytes 337928
  816.9 36.5 %collective-permute-start.5 = (f32[80,352]{1,0:T(8,128)S(1)}, f32[80,352]{1,0:T(8,128)S(1)}, u32[]{:S(2)}, u32[]{:S(2)}) collective-permute-start(f32[80,352]{1,0:T(8,128)S(1)} %fusion), channel_id=1, source_target_pairs={{0,72},{12,84},{24,96},{36,108},{48,120},{60,132},{72,144},{84,156... | collective-permute-start | bytes 337928
  835.8 20.8 %collective-permute-start.4 = (f32[80,352]{1,0:T(8,128)S(1)}, f32[80,352]{1,0:T(8,128)S(1)}, u32[]{:S(2)}, u32[]{:S(2)}) collective-permute-start(f32[80,352]{1,0:T(8,128)S(1)} %fusion), channel_id=1, source_target_pairs={{0,60},{12,72},{24,84},{36,96},{48,108},{60,120},{72,132},{84,144}... | collective-permute-start | bytes 337928
  837.1 19.6 %copy-start.3 = (f32[80,352]{1,0:T(8,128)}, f32[80,352]{1,0:T(8,128)S(1)}, u32[]{:S(2)}) copy-start(f32[80,352]{1,0:T(8,128)S(1)} %collective-permute-done.8) | copy-start | bytes 337924
  837.1 19.5 %collective-permute-start.3 = (f32[80,352]{1,0:T(8,128)S(1)}, f32[80,352]{1,0:T(8,128)S(1)}, u32[]{:S(2)}, u32[]{:S(2)}) collective-permute-start(f32[80,352]{1,0:T(8,128)S(1)} %fusion), channel_id=1, source_target_pairs={{0,48},{12,60},{24,72},{36,84},{48,96},{60,108},{72,120},{84,132},... | collective-permute-start | bytes 337928
  846.6 10.2 copy-start.4
  846.6 10.1 collective-permute-start.2
  847.9 8.8 copy-start.5
  847.9 8.8 collective-permute-start.1
  853.5 3.3 copy-start.6
  853.5 4.6 collective-permute-start
  856.6 0.7 copy-start.7
  856.7 0.7 copy-start.8
  856.7 0.7 copy-start.9
  857.4 0.7 copy-start.10
  868.1 253.4 %copy-start.2 = (bf16[192,352]{1,0:T(8,128)(2,1)S(1)}, bf16[192,352]{1,0:T(8,128)(2,1)}, u32[]{:S(2)}) copy-start(bf16[192,352]{1,0:T(8,128)(2,1)} %param.2) | copy-start | bytes 405508
  868.1 253.4 %copy-start.12 = (f32[352]{0:T(512)S(1)}, f32[352]{0:T(512)}, u32[]{:S(2)}) copy-start(f32[352]{0:T(512)} %copy-done.11) | copy-start | bytes 4228
  868.2 253.4 %copy-start.14 = (f32[352]{0:T(512)S(1)}, f32[352]{0:T(512)}, u32[]{:S(2)}) copy-start(f32[352]{0:T(512)} %copy-done.13) | copy-start | bytes 4228
  868.2 326.0 %reduce-scatter.6.cloned.1.call-start = ((), (), s32[]{:S(2)}) async-start(), calls=%async_computation.2 | async-start | bytes 2342912
  1127.3 3.1 copy-start.1
Sparse Core Ops, SparseCore 0:
  868.2 247.4 all-gather.2
  1127.4 66.6 reduce-scatter.5
where the time goes:
time: 1470 us; the launch traced here: 1440 us
  blocking collectives  1030 us (70%)
  waiting for transfers between devices  310 us (21%)
  starting transfers between devices  48 us (3%)
  local copies, waits for them, and re-layouts  23.1 us (2%)
  between operations  15.1 us (1%)
    psum x1, blocking collectives, local(): lax.psum((jnp.sum(first, axis=0), jnp.sum(first * first, axis=0), jnp.sum...  468 us
    unnamed x1, blocking collectives  322 us
    all_gather x1, waiting for transfers between devices, local(): piece = lax.all_gather(grad_t, 'dp', axis=0, tiled=True)  248 us
    psum x1, blocking collectives, local(): lax.psum((jnp.sum(total_a, axis=0), jnp.sum(total_a * norm_a, axis=0)), '...  239 us
    unnamed x15, waiting for transfers between devices  62.7 us
    unnamed x13, starting transfers between devices  47.9 us
  transfers between devices with their start and end apart: 14, of which 2 were waited for; matrix products, arithmetic and copies ran while one was open for 0% of the time, Pallas kernels for 0%

commit v1 on v0

v1 whole, which is shorter than its diff:
```python
import itertools

import jax
import jax.numpy as jnp
from jax import lax
from jax.experimental import pallas as pl
from jax.experimental.pallas import tpu as pltpu
from jax.sharding import PartitionSpec as P

EPS = 1e-05
WEIGHT = 0.0051
LANES = 128
CORES = 2
Z_HI = 2
X_CHIPS = 4
AXES = ("y", "zh", "x", "zl", "core")


def position(sizes):
    dp = lax.axis_index("dp")
    fs = lax.axis_index("fsdp")
    nx, nzh, nc = sizes["x"], sizes["zh"], sizes["core"]
    return {
        "x": dp % nx,
        "zh": (dp // nx) % nzh,
        "y": dp // (nx * nzh),
        "core": fs % nc,
        "zl": fs // nc,
    }


def device_of(place, sizes):
    dp = (place["y"] * sizes["zh"] + place["zh"]) * sizes["x"] + place["x"]
    return {"dp": dp, "fsdp": place["zl"] * sizes["core"] + place["core"]}


def exchange(src, axes, sizes, gather, collective_id):
    count = 1
    for a in axes:
        count *= sizes[a]
    piece = src.shape if gather else src.shape[1:]
    offsets = [o for o in itertools.product(*[range(sizes[a]) for a in axes]) if any(o)]

    def index(place):
        where = 0
        for a in axes:
            where = where * sizes[a] + place[a]
        return where

    def kernel(src_ref, dst_ref, send_sem, recv_sem, own_sem):
        here = position(sizes)
        me = index(here)
        peers = []
        for off in offsets:
            there = dict(here)
            for a, d in zip(axes, off):
                there[a] = (here[a] + d) % sizes[a]
            peers.append(there)
        barrier = pltpu.get_barrier_semaphore()
        for there in peers:
            pl.semaphore_signal(
                barrier,
                inc=1,
                device_id=device_of(there, sizes),
                device_id_type=pl.DeviceIdType.MESH,
            )
        own = pltpu.make_async_copy(
            src_ref if gather else src_ref.at[me], dst_ref.at[me], own_sem
        )
        own.start()
        pl.semaphore_wait(barrier, len(peers))
        copies = []
        for k, there in enumerate(peers):
            copy = pltpu.make_async_remote_copy(
                src_ref=src_ref if gather else src_ref.at[index(there)],
                dst_ref=dst_ref.at[me],
                send_sem=send_sem.at[k],
                recv_sem=recv_sem.at[k],
                device_id=device_of(there, sizes),
                device_id_type=pl.DeviceIdType.MESH,
            )
            copy.start()
            copies.append(copy)
        own.wait()
        for copy in copies:
            copy.wait()

    return pl.pallas_call(
        kernel,
        out_shape=jax.ShapeDtypeStruct((count,) + tuple(piece), src.dtype),
        in_specs=[pl.BlockSpec(memory_space=pl.ANY)],
        out_specs=pl.BlockSpec(memory_space=pl.ANY),
        scratch_shapes=[
            pltpu.SemaphoreType.DMA((len(offsets),)),
            pltpu.SemaphoreType.DMA((len(offsets),)),
            pltpu.SemaphoreType.DMA,
        ],
        compiler_params=pltpu.CompilerParams(
            collective_id=collective_id, has_side_effects=True
        ),
    )(src)


def local(z_a, z_b, sizes):
    rows, block = z_a.shape
    nx, ny, nzl, nc = sizes["x"], sizes["y"], sizes["zl"], sizes["core"]
    nf = nzl * nc
    batch = rows * nx * ny * sizes["zh"]
    lanes = -(-(block + 1) // LANES) * LANES
    per_x = nf // nx
    wide = per_x * lanes
    images = rows * nx
    slot = lanes // ny
    here = position(sizes)

    pad = ((0, 0), (0, lanes - block))
    mine = jnp.pad(z_a, pad)
    groups = []
    for x in range(nx):
        parts = [
            jnp.pad(z_b[:, f * block : (f + 1) * block], pad)
            for f in range(x * per_x, (x + 1) * per_x)
        ]
        groups.append(jnp.concatenate(parts + [mine], axis=1))
    raw = exchange(jnp.stack(groups), ("x",), sizes, False, 0).reshape(images, wide + lanes)
    raw = raw.astype(jnp.float32)

    sums = jnp.stack([jnp.sum(raw, axis=0), jnp.sum(raw * raw, axis=0)])
    every = exchange(jnp.pad(sums, ((0, 6), (0, 0))), ("y", "zh"), sizes, True, 1)
    sums = jnp.sum(every, axis=0) / batch
    center = sums[0]
    inverse = lax.rsqrt(sums[1] - center * center + EPS)
    norm = (raw - center) * inverse
    lane = jnp.arange(wide + lanes, dtype=jnp.int32) % lanes
    low = jnp.where(lane == block, 1.0, norm).astype(jnp.bfloat16)
    low_b, low_a = low[:, :wide], low[:, wide:]

    part = lax.dot_general(
        low_a, low_b, (((0,), (0,)), ((), ())), preferred_element_type=jnp.float32
    )
    got = exchange(
        part.astype(jnp.bfloat16).reshape(ny, slot, wide), ("y",), sizes, False, 2
    )
    owned = jnp.sum(got.astype(jnp.float32), axis=0)
    both = exchange(owned.astype(jnp.bfloat16), ("zh",), sizes, True, 3)
    corr = (
        owned
        + lax.dynamic_index_in_dim(both, 1 - here["zh"], 0, False).astype(jnp.float32)
    ) / batch

    row0 = (here["zl"] * nc + here["core"]) * lanes
    col0 = here["x"] * wide

    def diagonal(first_row, shape):
        row = first_row + lax.broadcasted_iota(jnp.int32, shape, 0)
        col = col0 + lax.broadcasted_iota(jnp.int32, shape, 1)
        return row == col

    grad = jnp.where(
        diagonal(row0 + here["y"] * slot, corr.shape),
        -2.0 * (1.0 - corr),
        2.0 * WEIGHT * corr,
    ).astype(jnp.bfloat16)
    grad = exchange(grad, ("y",), sizes, True, 4).reshape(lanes, wide)

    wide_g = grad.astype(jnp.float32)
    mean_b = wide_g[block, :] / (2.0 * WEIGHT)
    mean_a = wide_g[:, block] / (2.0 * WEIGHT)
    real = (lax.broadcasted_iota(jnp.int32, grad.shape, 0) < block) & (
        lax.broadcasted_iota(jnp.int32, grad.shape, 1) % lanes < block
    )
    wide_g = jnp.where(real, wide_g, 0.0)
    grad = wide_g.astype(jnp.bfloat16)
    back_corr = jnp.where(
        diagonal(row0, grad.shape), 1.0 + 0.5 * wide_g, wide_g / (2.0 * WEIGHT)
    )
    cross = wide_g * back_corr
    flat_a = jnp.sum(wide_g * mean_b[None, :], axis=1)
    flat_b = jnp.sum(wide_g * mean_a[:, None], axis=0)
    cross_a = jnp.sum(cross, axis=1)
    cross_b = jnp.sum(cross, axis=0)
    part_a = lax.dot_general(
        low_b, grad, (((1,), (1,)), ((), ())), preferred_element_type=jnp.float32
    )
    part_b = jnp.dot(low_a, grad, preferred_element_type=jnp.float32)
    part_a = part_a - flat_a - norm[:, wide:] * cross_a
    part_b = part_b - flat_b - norm[:, :wide] * cross_b
    both_parts = (jnp.concatenate([part_b, part_a], axis=1) * inverse).astype(jnp.bfloat16)
    got = exchange(
        both_parts.reshape(nx, rows, wide + lanes), ("x",), sizes, False, 5
    )
    total_a = jnp.sum(got[:, :, wide:].astype(jnp.float32), axis=0)
    grad_a = total_a[:, :block].astype(jnp.bfloat16)

    pieces = got[:, :, :wide].reshape(nx, rows, per_x, lanes)
    pieces = jnp.transpose(pieces, (0, 2, 1, 3)).reshape(nzl, nc, rows, lanes)
    pieces = jnp.transpose(pieces, (1, 0, 2, 3))
    pair = exchange(pieces, ("core",), sizes, False, 6)
    pair = jnp.sum(pair.astype(jnp.float32), axis=0).astype(jnp.bfloat16)
    line = exchange(pair, ("zl",), sizes, False, 7)
    total_b = jnp.sum(line.astype(jnp.float32), axis=0)
    grad_b = total_b[:, :block].astype(jnp.bfloat16)
    return grad_a, grad_b


def solution(mesh):
    fsdp, dp = mesh.shape["fsdp"], mesh.shape["dp"]
    sizes = {
        "core": CORES,
        "zl": fsdp // CORES,
        "x": X_CHIPS,
        "zh": Z_HI,
        "y": dp // (X_CHIPS * Z_HI),
    }
    return jax.shard_map(
        lambda z_a, z_b: local(z_a, z_b, sizes),
        mesh=mesh,
        in_specs=(P("dp", "fsdp"), P("dp", None)),
        out_specs=(P("dp", "fsdp"), P("dp", "fsdp")),
        check_vma=False,
    )
```

time: 1470 us -> 285 us (0.19)
  the two profiles are of different devices: /device:TPU:1 before, /device:TPU:137 now
where the time goes in v1:
time: 285 us
  Pallas kernels  240 us (84%)
  other arithmetic  24.3 us (9%)
  local copies, waits for them, and re-layouts  10.8 us (4%)
  matrix products  8.73 us (3%)
    pallas_call x8, Pallas kernels, exchange(): pl.pallas_call(kernel, out_shape=jax.ShapeDtypeStruct((count,) + tuple(pi...  240 us

profile of v1, /device:TPU:137, one launch (start us, length us, event | category | flops | bytes accessed | tf_op | source)
XLA Modules:
  0.0 284.8 jit_solution(16692758390801382412)
XLA Ops:
  0.7 2.2 fusion.51
  2.9 0.9 slice_select_fusion
  4.1 1.7 pad_maximum_fusion.src_ref
  5.8 30.2 %shard_map.41 = bf16[4,192,1536]{2,1,0:T(8,128)(2,1)} custom-call(bf16[4,192,1536]{2,1,0:T(8,128)(2,1)} %pad_maximum_fusion.src_ref), custom_call_target="tpu_custom_call" | custom-call | tf_op jit(solution)/shard_map/pallas_call | solution.py:88
  36.0 2.5 convert_reduce_fusion
  38.5 0.6 select_maximum_fusion.2.src_ref
  39.1 38.5 %shard_map.42 = f32[16,8,1536]{2,1,0:T(8,128)} custom-call(f32[8,1536]{1,0:T(8,128)} %select_maximum_fusion.2.src_ref), custom_call_target="tpu_custom_call" | custom-call | tf_op jit(solution)/shard_map/pallas_call | solution.py:88
  77.7 1.2 reduce_sum.104
  78.9 3.0 %fusion.1 = (f32[768,1536]{1,0:T(8,128)}, bf16[768,1536]{1,0:T(8,128)(2,1)S(1)}) fusion(bf16[4,192,1536]{2,1,0:T(8,128)(2,1)S(1)} %copy-done, f32[1536]{0:T(1024)S(1)} %get-tuple-element.9, f32[1536]{0:T(1024)S(1)} %get-tuple-element.8, pred[1536]{0:T(1024)(128)(4,1)S(1)} %fusion.39), kind=kLoop, calls=%fused_computation.3 | loop fusion | flops 5898240 | bytes 9451008 | tf_op jit(solution)/shard_map/mul | solution.py:133
  81.9 1.9 convolution_convert_fusion
  83.8 27.3 %shard_map.43 = bf16[8,48,1152]{2,1,0:T(8,128)(2,1)} custom-call(bf16[8,48,1152]{2,1,0:T(8,128)(2,1)} %bitcast.39), custom_call_target="tpu_custom_call" | custom-call | tf_op jit(solution)/shard_map/pallas_call | solution.py:88
  111.1 1.3 convert_reduce_fusion.1
  112.4 0.7 convert_element_type.82.src_ref
  113.0 11.8 %shard_map.44 = bf16[2,48,1152]{2,1,0:T(8,128)(2,1)} custom-call(bf16[48,1152]{1,0:T(8,128)(2,1)} %convert_element_type.82.src_ref), custom_call_target="tpu_custom_call" | custom-call | tf_op jit(solution)/shard_map/pallas_call | solution.py:88
  125.0 1.6 select_convert_fusion.2.src_ref
  126.6 25.6 %shard_map.45 = bf16[8,48,1152]{2,1,0:T(8,128)(2,1)} custom-call(bf16[48,1152]{1,0:T(8,128)(2,1)} %select_convert_fusion.2.src_ref), custom_call_target="tpu_custom_call" | custom-call | tf_op jit(solution)/shard_map/pallas_call | solution.py:88
  152.2 1.4 bitcast_convert_fusion
  154.0 1.2 fusion.22
  155.6 3.6 %fusion.2 = f32[768,1152]{1,0:T(8,128)S(1)} fusion(bf16[384,1152]{1,0:T(8,128)(2,1)S(1)} %select_convert_fusion.1, f32[768,1536]{1,0:T(8,128)} %get-tuple-element.10, f32[1152]{0:T(1024)S(1)} %get-tuple-element.4, f32[1152]{0:T(1024)S(1)} %get-tuple-element.6, bf16[768,1536]{1,0:T(8,128)(2,1)} %copy-done.3), kind=kOutput, calls=%fused_computation.7 | convolution fusion | flops 682131456 | bytes 8561664 | tf_op jit(solution)/shard_map/dot_general | solution.py:185
  159.2 0.7 mul.128
  160.0 3.2 %fusion.12 = f32[768,384]{1,0:T(8,128)S(1)} fusion(bf16[384,1152]{1,0:T(8,128)(2,1)} %copy-done.4, bf16[768,1536]{1,0:T(8,128)(2,1)} %copy-done.3, f32[768,1536]{1,0:T(8,128)} %get-tuple-element.10, f32[384]{0:T(512)} %mul.128, f32[384]{0:T(512)S(1)} %sub.70), kind=kOutput, calls=%fused_computation.31 | convolution fusion | flops 680361984 | bytes 5017088 | tf_op jit(solution)/shard_map/dot_general | solution.py:182
  163.2 1.8 fusion.src_ref
  165.0 28.8 %shard_map.46 = bf16[4,192,1536]{2,1,0:T(8,128)(2,1)} custom-call(bf16[4,192,1536]{2,1,0:T(8,128)(2,1)} %fusion.src_ref), custom_call_target="tpu_custom_call" | custom-call | tf_op jit(solution)/shard_map/pallas_call | solution.py:88
  193.7 1.5 slice-done
  195.2 2.6 reshape.146
  197.8 2.0 copy.5
  199.8 1.4 copy.9
  201.2 28.7 %shard_map.47 = bf16[2,6,192,384]{3,2,1,0:T(8,128)(2,1)} custom-call(bf16[2,6,192,384]{3,2,1,0:T(8,128)(2,1)} %bitcast.36), custom_call_target="tpu_custom_call" | custom-call | tf_op jit(solution)/shard_map/pallas_call | solution.py:88
  229.9 2.9 %reduce_sum.111.src_ref = bf16[6,192,384]{2,1,0:T(8,128)(2,1)} reduce(bf16[2,6,192,384]{3,2,1,0:T(8,128)(2,1)} %shard_map.47, bf16[]{:T(256)} %constant.110.clone.1), dimensions={0}, to_apply=%region_9.10 | reduce | flops 442368 | bytes 2654210 | tf_op jit(solution)/shard_map/reduce_sum | solution.py:199
  232.8 49.2 %shard_map.48 = bf16[6,192,384]{2,1,0:T(8,128)(2,1)} custom-call(bf16[6,192,384]{2,1,0:T(8,128)(2,1)} %reduce_sum.111.src_ref), custom_call_target="tpu_custom_call" | custom-call | tf_op jit(solution)/shard_map/pallas_call | solution.py:88
  282.1 2.0 reduce.8
  284.1 0.7 slice_reduce_fusion
  (35 shorter events, 1.2 us)
Async XLA Ops:
  0.6 2.2 copy-start.6
  0.6 3.2 %copy-start.5 = (bf16[192,352]{1,0:T(8,128)(2,1)S(1)}, bf16[192,352]{1,0:T(8,128)(2,1)}, u32[]{:S(2)}) copy-start(bf16[192,352]{1,0:T(8,128)(2,1)} %param.2) | copy-start | bytes 405508
  36.0 43.0 %copy-start = (bf16[4,192,1536]{2,1,0:T(8,128)(2,1)S(1)}, bf16[4,192,1536]{2,1,0:T(8,128)(2,1)}, u32[]{:S(2)}) copy-start(bf16[4,192,1536]{2,1,0:T(8,128)(2,1)} %shard_map.41) | copy-start | bytes 7077892
  81.9 1.9 copy-start.3
  152.2 1.4 copy-start.1
  155.6 3.7 %copy-start.4 = (bf16[384,1152]{1,0:T(8,128)(2,1)}, bf16[384,1152]{1,0:T(8,128)(2,1)S(1)}, u32[]{:S(2)}) copy-start(bf16[384,1152]{1,0:T(8,128)(2,1)S(1)} %select_convert_fusion.1) | copy-start | bytes 2654212
  193.7 1.5 slice-start
  232.8 51.2 %copy-start.2 = (bf16[4,192,1536]{2,1,0:T(8,128)(2,1)S(1)}, bf16[4,192,1536]{2,1,0:T(8,128)(2,1)}, u32[]{:S(2)}) copy-start(bf16[4,192,1536]{2,1,0:T(8,128)(2,1)} %shard_map.46) | copy-start | bytes 7077892

commit v2 on v0

v2 whole, which is shorter than its diff:
```python
import jax
import jax.numpy as jnp
from jax import lax
from jax.experimental import pallas as pl
from jax.experimental.pallas import tpu as pltpu
from jax.sharding import PartitionSpec as P

EPS = 1e-05
WEIGHT = 0.0051
LANES = 128
CORES = 2
Z_HI = 2
X_CHIPS = 4
SUB = 4
MESH = pl.DeviceIdType.MESH
F32 = jnp.float32
BF16 = jnp.bfloat16


class Plan:
    def __init__(self, mesh, rows, block):
        fsdp, dp = mesh.shape["fsdp"], mesh.shape["dp"]
        self.nx, self.nh, self.nc = X_CHIPS, Z_HI, CORES
        self.ny = dp // (self.nx * self.nh)
        self.nz = fsdp // self.nc
        self.nf = fsdp
        self.nq = self.nf // self.nx
        self.rows, self.block = rows, block
        self.lanes = -(-(block + 1) // LANES) * LANES
        self.slot = self.lanes // self.ny
        self.batch = rows * dp
        self.right = self.ny // 2
        self.left = self.ny - 1 - self.right


class Copies:
    def __init__(self):
        self.count = 0

    def take(self, n=1):
        first = self.count
        self.count += n
        return first


def build(p):
    copies = Copies()
    nx, ny, nh, nz, nc, nq = p.nx, p.ny, p.nh, p.nz, p.nc, p.nq
    rows, lanes, slot, block = p.rows, p.lanes, p.slot, p.block
    half = rows // nc
    part = rows // SUB
    marks = dict(
        a=copies.take(nx),
        b=copies.take(nx * nq),
        pass_b=copies.take(nx * nq),
        stat_x=copies.take(nx),
        stat_y=copies.take(ny),
        stat_h=copies.take(nh),
        rs_r=copies.take(p.right * nq),
        rs_l=copies.take(p.left * nq),
        swap=copies.take(nq),
        ag_r=copies.take(p.right * nq),
        ag_l=copies.take(p.left * nq),
        pair=copies.take((nx // nc) * nq),
        back_a=copies.take(nx),
        chain_r=copies.take(nz * SUB),
        chain_l=copies.take(nz * SUB),
        final=copies.take(1),
    )

    def kernel(
        za,
        zb,
        out_a,
        out_b,
        raw_a,
        raw_b,
        pack,
        low_a,
        low_b,
        low_t,
        stat_x,
        stat_y,
        stat_h,
        mean,
        tile,
        rs_rin,
        rs_rout,
        rs_lin,
        rs_lout,
        owned,
        swap_out,
        swap_in,
        grad,
        acc_a,
        send_a,
        recv_a,
        blocks,
        pair,
        chain_rin,
        chain_rout,
        chain_lin,
        chain_lout,
        done_out,
        done_in,
        send_sem,
        recv_sem,
        own_sem,
    ):
        dp = lax.axis_index("dp")
        fs = lax.axis_index("fsdp")
        x = dp % nx
        h = (dp // nx) % nh
        y = dp // (nx * nh)
        core = fs % nc
        zl = fs // nc

        def device(x=x, y=y, h=h, zl=zl, core=core):
            return {"dp": (y * nh + h) * nx + x, "fsdp": zl * nc + core}

        def remote(src, dst, mark, there):
            return pltpu.make_async_remote_copy(
                src_ref=src,
                dst_ref=dst,
                send_sem=send_sem.at[mark],
                recv_sem=recv_sem.at[mark],
                device_id=there,
                device_id_type=MESH,
            )

        q_own = zl % nq
        to_x = (zl // nq) * nc + core
        to_f = nq * x + q_own
        from_x = fs // nq
        from_q = fs % nq
        from_z = (x // nc) * nq + from_q
        stays = (to_x == x) & (to_f == fs)

        barrier = pltpu.get_barrier_semaphore()

        def greet(there):
            pl.semaphore_signal(barrier, inc=1, device_id=there, device_id_type=MESH)

        for k in range(1, nx):
            greet(device(x=(x + k) % nx))
        for k in range(1, ny):
            greet(device(y=(y + k) % ny))
        greet(device(h=1 - h))
        greet(device(core=1 - core))
        greet(device(zl=(zl + 1) % nz))
        greet(device(zl=(zl + nz - 1) % nz))

        @pl.when(jnp.logical_not(stays))
        def _():
            greet(device(x=from_x, zl=from_z, core=x % nc))

        waiting = []

        zero = jnp.zeros((rows, lanes - block), BF16)
        raw_a[x] = jnp.concatenate([za[...], zero], axis=1)
        for f in range(p.nf):
            piece = zb[:, f * block : (f + 1) * block]
            pack[f // nq, f % nq] = jnp.concatenate([piece, zero], axis=1)

        pl.semaphore_wait(barrier, nx - 1 + ny - 1 + 4 + jnp.where(stays, 0, 1))

        def start(copy):
            copy.start()
            waiting.append(copy)
            return copy

        into_a = {}
        for k in range(1, nx):
            into_a[k] = start(
                remote(
                    raw_a.at[x], raw_a.at[x], marks["a"] + k, device(x=(x + k) % nx)
                )
            )
        own_rows = pl.ds(core * half, half)
        into_b = {}
        for q in range(nq):
            for k in range(1, nx):
                t = (x + k) % nx
                into_b[q, k] = start(
                    remote(
                        pack.at[t, q, own_rows],
                        raw_b.at[q, x, own_rows],
                        marks["b"] + q * nx + k,
                        device(x=t),
                    )
                )
        mine = []
        for q in range(nq):
            copy = pltpu.make_async_copy(pack.at[x, q], raw_b.at[q, x], own_sem.at[q])
            copy.start()
            mine.append(copy)

        def sums(value):
            v = value.astype(F32)
            return (
                jnp.sum(v, axis=0, keepdims=True),
                jnp.sum(v * v, axis=0, keepdims=True),
            )

        first = [sums(pack[f // nq, f % nq]) for f in range(p.nf)]
        first_a = sums(raw_a[x])
        for t in range(nx):
            both = first[t * nq : (t + 1) * nq] + [first_a]
            stat_x[0, t] = jnp.concatenate(
                [s for s, _ in both] + [s for _, s in both], axis=0
            )
        got = []
        for k in range(1, nx):
            t = (x + k) % nx
            got.append(
                start(
                    remote(
                        stat_x.at[0, t],
                        stat_x.at[1, k],
                        marks["stat_x"] + k,
                        device(x=t),
                    )
                )
            )
        total = stat_x[0, x]
        for k in range(1, nx):
            got[k - 1].wait_recv()
            total = total + stat_x[1, k]
        stat_y[0] = total
        got = []
        for k in range(1, ny):
            got.append(
                start(
                    remote(
                        stat_y.at[0],
                        stat_y.at[k],
                        marks["stat_y"] + k,
                        device(y=(y + k) % ny),
                    )
                )
            )
        for k in range(1, ny):
            got[k - 1].wait_recv()
            total = total + stat_y[k]
        stat_h[0] = total
        swap = start(
            remote(stat_h.at[0], stat_h.at[1], marks["stat_h"], device(h=1 - h))
        )
        swap.wait_recv()
        total = (total + stat_h[1]) / p.batch
        count = nq + 1
        center = total[:count]
        inverse = lax.rsqrt(total[count:] - center * center + EPS)
        mean[:count] = center
        mean[count:] = inverse

        lane = lax.broadcasted_iota(jnp.int32, (rows, lanes), 1)

        def normal(raw, which):
            v = raw.astype(F32)
            return (v - mean[which : which + 1, :]) * mean[
                count + which : count + which + 1, :
            ]

        def low(raw, which):
            return jnp.where(lane == block, 1.0, normal(raw, which)).astype(BF16)

        for k in range(1, nx):
            into_a[k].wait_recv()

        def low_a_step(i, _):
            low_a[i] = low(raw_a[i], nq)
            return 0

        lax.fori_loop(0, nx, low_a_step, 0)
        for i in range(nx):
            low_t[:, i * rows : (i + 1) * rows] = jnp.transpose(
                low_a[i].astype(F32)
            ).astype(BF16)

        passed = {}
        for q in range(nq):
            for k in range(1, nx):
                into_b[q, k].wait_recv()
                s = (x + nx - k) % nx
                passed[q, k] = start(
                    remote(
                        raw_b.at[q, s, own_rows],
                        raw_b.at[q, s, own_rows],
                        marks["pass_b"] + q * nx + k,
                        device(core=1 - core),
                    )
                )

        right, left = device(y=(y + 1) % ny), device(y=(y + ny - 1) % ny)

        def ring(src, dst, name, step, q, there):
            return start(remote(src, dst, marks[name] + step * nq + q, there))

        rs_r, rs_l = {}, {}
        for q in range(nq):
            mine[q].wait()
            for k in range(1, nx):
                passed[q, k].wait_recv()

            def low_b_step(i, _):
                low_b[q, i] = low(raw_b[q, i], q)
                return 0

            lax.fori_loop(0, nx, low_b_step, 0)
            product = jnp.dot(
                low_t[...],
                low_b[q].reshape(nx * rows, lanes),
                preferred_element_type=F32,
            )
            tile[q] = product.astype(BF16).reshape(ny, slot, lanes)
            rs_r[0, q] = ring(
                tile.at[q, (y + p.right) % ny], rs_rin.at[0, q], "rs_r", 0, q, right
            )
            rs_l[0, q] = ring(
                tile.at[q, (y + ny - p.left) % ny], rs_lin.at[0, q], "rs_l", 0, q, left
            )

        for s in range(1, p.right):
            for q in range(nq):
                t = (y + p.right - s) % ny
                rs_r[s - 1, q].wait_recv()
                rs_rout[s, q] = (
                    rs_rin[s - 1, q].astype(F32) + tile[q, t].astype(F32)
                ).astype(BF16)
                rs_r[s, q] = ring(
                    rs_rout.at[s, q], rs_rin.at[s, q], "rs_r", s, q, right
                )
                if s < p.left:
                    t = (y + ny - p.left + s) % ny
                    rs_l[s - 1, q].wait_recv()
                    rs_lout[s, q] = (
                        rs_lin[s - 1, q].astype(F32) + tile[q, t].astype(F32)
                    ).astype(BF16)
                    rs_l[s, q] = ring(
                        rs_lout.at[s, q], rs_lin.at[s, q], "rs_l", s, q, left
                    )
        swaps = {}
        for q in range(nq):
            rs_l[p.left - 1, q].wait_recv()
            rs_r[p.right - 1, q].wait_recv()
            value = (
                tile[q, y].astype(F32)
                + rs_rin[p.right - 1, q].astype(F32)
                + rs_lin[p.left - 1, q].astype(F32)
            )
            owned[q] = value
            swap_out[q] = value.astype(BF16)
            swaps[q] = start(
                remote(
                    swap_out.at[q], swap_in.at[q], marks["swap"] + q, device(h=1 - h)
                )
            )

        ag_r, ag_l = {}, {}
        for q in range(nq):
            swaps[q].wait_recv()
            corr = (owned[q] + swap_in[q].astype(F32)) / p.batch
            row = y * slot + lax.broadcasted_iota(jnp.int32, (slot, lanes), 0)
            col = lax.broadcasted_iota(jnp.int32, (slot, lanes), 1)
            on = (row == col) & (fs == nq * x + q)
            grad[q, y] = jnp.where(
                on, -2.0 * (1.0 - corr), 2.0 * WEIGHT * corr
            ).astype(BF16)
            ag_r[0, q] = ring(grad.at[q, y], grad.at[q, y], "ag_r", 0, q, right)
            ag_l[0, q] = ring(grad.at[q, y], grad.at[q, y], "ag_l", 0, q, left)
        for s in range(1, p.right):
            for q in range(nq):
                ag_r[s - 1, q].wait_recv()
                t = (y + ny - s) % ny
                ag_r[s, q] = ring(grad.at[q, t], grad.at[q, t], "ag_r", s, q, right)
                if s < p.left:
                    ag_l[s - 1, q].wait_recv()
                    t = (y + s) % ny
                    ag_l[s, q] = ring(grad.at[q, t], grad.at[q, t], "ag_l", s, q, left)
        for q in range(nq):
            ag_r[p.right - 1, q].wait_recv()
            ag_l[p.left - 1, q].wait_recv()

        row = lax.broadcasted_iota(jnp.int32, (lanes, lanes), 0)
        col = lax.broadcasted_iota(jnp.int32, (lanes, lanes), 1)
        real = (row < block) & (col < block)
        flat_a = jnp.zeros((1, lanes), F32)
        cross_a = jnp.zeros((1, lanes), F32)
        pairs = {}
        for q in range(nq):
            g = grad[q].reshape(lanes, lanes).astype(F32)
            mean_b = g[block : block + 1, :] / (2.0 * WEIGHT)
            mean_a = g[:, block : block + 1] / (2.0 * WEIGHT)
            g = jnp.where(real, g, 0.0)
            on = (row == col) & (fs == nq * x + q)
            cross = g * jnp.where(on, 1.0 + 0.5 * g, g / (2.0 * WEIGHT))
            flat_b = jnp.sum(g * mean_a, axis=0, keepdims=True)
            cross_b = jnp.sum(cross, axis=0, keepdims=True)
            flat_a += jnp.sum(jnp.transpose(g * mean_b), axis=0, keepdims=True)
            cross_a += jnp.sum(jnp.transpose(cross), axis=0, keepdims=True)
            g = g.astype(BF16)

            def back_b_step(i, _):
                value = jnp.dot(low_a[i], g, preferred_element_type=F32)
                value = value - flat_b - normal(raw_b[q, i], q) * cross_b
                blocks[i, q] = (value * mean[count + q : count + q + 1, :]).astype(BF16)
                return 0

            lax.fori_loop(0, nx, back_b_step, 0)
            for m in range(nx // nc):
                pairs[m, q] = start(
                    remote(
                        blocks.at[m * nc + 1 - core, q],
                        pair.at[m, q],
                        marks["pair"] + m * nq + q,
                        device(core=1 - core),
                    )
                )

            def back_a_step(i, _):
                value = lax.dot_general(
                    low_b[q, i], g, (((1,), (1,)), ((), ())), preferred_element_type=F32
                )
                acc_a[i] = value if q == 0 else acc_a[i] + value
                return 0

            lax.fori_loop(0, nx, back_a_step, 0)

        inv_a = mean[count + nq : count + nq + 1, :]

        def close_a_step(i, _):
            value = acc_a[i] - flat_a - normal(raw_a[i], nq) * cross_a
            value = value * inv_a
            acc_a[i] = value
            send_a[i] = value.astype(BF16)
            return 0

        lax.fori_loop(0, nx, close_a_step, 0)
        backs = []
        for k in range(1, nx):
            t = (x + k) % nx
            backs.append(
                start(
                    remote(
                        send_a.at[t], recv_a.at[k], marks["back_a"] + k, device(x=t)
                    )
                )
            )
        for m in range(nx // nc):
            for q in range(nq):
                pairs[m, q].wait_recv()

        def own(d, s):
            m, q = d // nq, d % nq
            at = pl.ds(s * part, part)
            return blocks[m * nc + core, q, at].astype(F32) + pair[m, q, at].astype(F32)

        def hop(src, dst, name, d, s, step):
            return remote(
                src.at[d, s],
                dst.at[d, s],
                marks[name] + d * SUB + s,
                device(zl=(zl + step + nz) % nz),
            )

        def hop_r(d, s):
            return hop(chain_rout, chain_rin, "chain_r", d, s, 1)

        def hop_l(d, s):
            return hop(chain_lout, chain_lin, "chain_l", d, s, -1)

        def chain(make, inbox, outbox, target, steps, starts):
            def step(i, _):
                d = target(i)
                for s in range(SUB):

                    @pl.when(starts)
                    def _():
                        outbox[d, s] = own(d, s).astype(BF16)

                    @pl.when(jnp.logical_not(starts))
                    def _():
                        make(d, s).wait_recv()
                        outbox[d, s] = (own(d, s) + inbox[d, s].astype(F32)).astype(
                            BF16
                        )

                    make(d, s).start()
                return 0

            lax.fori_loop(0, steps, step, 0)

        def chain_end(make, target, steps):
            def step(i, _):
                for s in range(SUB):
                    make(target(i), s).wait_send()
                return 0

            lax.fori_loop(0, steps, step, 0)

        def chain_right():
            chain(
                hop_r,
                chain_rin,
                chain_rout,
                lambda i: nz - 1 - i,
                nz - 1 - zl,
                zl == 0,
            )

        def chain_left():
            chain(hop_l, chain_lin, chain_lout, lambda i: i, zl, zl == nz - 1)

        low_half = zl < nz // 2

        @pl.when(low_half)
        def _():
            chain_right()
            chain_left()

        @pl.when(jnp.logical_not(low_half))
        def _():
            chain_left()
            chain_right()

        total_a = acc_a[x]
        for k in range(1, nx):
            backs[k - 1].wait_recv()
            total_a = total_a + recv_a[k].astype(F32)
        out_a[...] = total_a[:, :block].astype(BF16)

        for s in range(SUB):
            at = pl.ds(s * part, part)
            acc_a[0, at] = own(zl, s)

            @pl.when(zl > 0)
            def _():
                hop_r(zl, s).wait_recv()
                acc_a[0, at] += chain_rin[zl, s].astype(F32)

            @pl.when(zl < nz - 1)
            def _():
                hop_l(zl, s).wait_recv()
                acc_a[0, at] += chain_lin[zl, s].astype(F32)

        done_out[...] = acc_a[0].astype(BF16)
        last = remote(
            done_out,
            done_in,
            marks["final"],
            device(x=to_x, zl=to_f // nc, core=to_f % nc),
        )

        @pl.when(stays)
        def _():
            out_b[...] = done_out[:, :block]

        @pl.when(jnp.logical_not(stays))
        def _():
            last.start()
            last.wait()
            out_b[...] = done_in[:, :block]

        chain_end(hop_r, lambda i: nz - 1 - i, nz - 1 - zl)
        chain_end(hop_l, lambda i: i, zl)
        for copy in waiting:
            copy.wait_send()

    vmem = pltpu.VMEM
    count = nq + 1
    shapes = [
        vmem((nx, rows, lanes), BF16),
        vmem((nq, nx, rows, lanes), BF16),
        vmem((nx, nq, rows, lanes), BF16),
        vmem((nx, rows, lanes), BF16),
        vmem((nq, nx, rows, lanes), BF16),
        vmem((lanes, nx * rows), BF16),
        vmem((2, nx, 2 * count, lanes), F32),
        vmem((ny, 2 * count, lanes), F32),
        vmem((2, 2 * count, lanes), F32),
        vmem((2 * count, lanes), F32),
        vmem((nq, ny, slot, lanes), BF16),
        vmem((p.right, nq, slot, lanes), BF16),
        vmem((p.right, nq, slot, lanes), BF16),
        vmem((max(p.left, 1), nq, slot, lanes), BF16),
        vmem((max(p.left, 1), nq, slot, lanes), BF16),
        vmem((nq, slot, lanes), F32),
        vmem((nq, slot, lanes), BF16),
        vmem((nq, slot, lanes), BF16),
        vmem((nq, ny, slot, lanes), BF16),
        vmem((nx, rows, lanes), F32),
        vmem((nx, rows, lanes), BF16),
        vmem((nx, rows, lanes), BF16),
        vmem((nx, nq, rows, lanes), BF16),
        vmem((nx // nc, nq, rows, lanes), BF16),
        vmem((nz, SUB, part, lanes), BF16),
        vmem((nz, SUB, part, lanes), BF16),
        vmem((nz, SUB, part, lanes), BF16),
        vmem((nz, SUB, part, lanes), BF16),
        vmem((rows, lanes), BF16),
        vmem((rows, lanes), BF16),
        pltpu.SemaphoreType.DMA((copies.count,)),
        pltpu.SemaphoreType.DMA((copies.count,)),
        pltpu.SemaphoreType.DMA((nq,)),
    ]
    result = jax.ShapeDtypeStruct((rows, block), BF16)
    return pl.pallas_call(
        kernel,
        out_shape=(result, result),
        in_specs=[pl.BlockSpec(memory_space=vmem)] * 2,
        out_specs=(pl.BlockSpec(memory_space=vmem),) * 2,
        scratch_shapes=shapes,
        compiler_params=pltpu.CompilerParams(
            collective_id=0, has_side_effects=True, vmem_limit_bytes=56 << 20
        ),
    )


def solution(mesh):
    def local(z_a, z_b):
        return build(Plan(mesh, *z_a.shape))(z_a, z_b)

    return jax.shard_map(
        local,
        mesh=mesh,
        in_specs=(P("dp", "fsdp"), P("dp", None)),
        out_specs=(P("dp", "fsdp"), P("dp", "fsdp")),
        check_vma=False,
    )
```

time: 1470 us -> 143 us (0.10); the launches traced: 1440 us -> 143 us
  blocking collectives: 1030 us -> 0 us
  waiting for transfers between devices: 310 us -> 0 us
  Pallas kernels: 0 us -> 139 us
  starting transfers between devices: 48 us -> 0 us
  local copies, waits for them, and re-layouts: 23.1 us -> 3.17 us
    psum x2 -> x0, blocking collectives: 707 us -> none  [the longest x1 468 us: local(): lax.psum((jnp.sum(first, axis=0), jnp.sum(first * first, axis=0), jnp.sum...]
    unnamed x1 -> x0, blocking collectives: 322 us -> none
    all_gather x1 -> x0, waiting for transfers between devices: 248 us -> none  [local(): piece = lax.all_gather(grad_t, 'dp', axis=0, tiled=True)]
    pallas_call x0 -> x1, Pallas kernels: none -> 139 us  [local(): return build(Plan(mesh, *z_a.shape))(z_a, z_b)]
    unnamed x15 -> x0, waiting for transfers between devices: 62.7 us -> none
    unnamed x13 -> x0, starting transfers between devices: 47.9 us -> none
    unnamed x36 -> x2, local copies, waits for them, and re-layouts: 23 us -> 3.17 us
  transfers between devices with their start and end apart: 14 -> 0, of which waited for: 2 -> 0; matrix products, arithmetic and copies ran while one was open for 0% -> 0% of each run, Pallas kernels for 0% -> 0%
where the time goes in v2:
time: 143 us
  Pallas kernels  139 us (97%)
  local copies, waits for them, and re-layouts  3.17 us (2%)
    pallas_call x1, Pallas kernels, local(): return build(Plan(mesh, *z_a.shape))(z_a, z_b)  139 us
    unnamed x2, local copies, waits for them, and re-layouts  3.17 us

profile of v2, /device:TPU:1, one launch (start us, length us, event | category | flops | bytes accessed | tf_op | source)
XLA Modules:
  0.0 142.9 jit_solution(16374940177361839515)
XLA Ops:
  0.6 139.0 %shard_map.41 = (bf16[192,352]{1,0:T(8,128)(2,1)}, bf16[192,352]{1,0:T(8,128)(2,1)}) custom-call(bf16[192,352]{1,0:T(8,128)(2,1)} %za.1, bf16[192,4224]{1,0:T(8,128)(2,1)} %zb.1), custom_call_target="tpu_custom_call" | custom-call | tf_op jit(solution)/shard_map/pallas_call | solution.py:622
  139.7 1.6 %copy.6 = bf16[192,352]{1,0:T(8,128)(2,1)} copy(bf16[192,352]{1,0:T(8,128)(2,1)} %get-tuple-element.4) | data formatting | bytes 270336
  141.3 1.6 %copy.7 = bf16[192,352]{1,0:T(8,128)(2,1)} copy(bf16[192,352]{1,0:T(8,128)(2,1)} %get-tuple-element.5) | data formatting | bytes 270336

commit v3 on v2

v3 whole, which is shorter than its diff:
```python
import jax
import jax.numpy as jnp
from jax import lax
from jax.experimental import pallas as pl
from jax.experimental.pallas import tpu as pltpu
from jax.sharding import PartitionSpec as P

EPS = 1e-05
WEIGHT = 0.0051
LANES = 128
CORES = 2
Z_HI = 2
X_CHIPS = 4
SUB = 4
MESH = pl.DeviceIdType.MESH
F32 = jnp.float32
BF16 = jnp.bfloat16


class Plan:
    def __init__(self, mesh, rows, block):
        fsdp, dp = mesh.shape["fsdp"], mesh.shape["dp"]
        self.nx, self.nh, self.nc = X_CHIPS, Z_HI, CORES
        self.ny = dp // (self.nx * self.nh)
        self.nz = fsdp // self.nc
        self.nf = fsdp
        self.nq = self.nf // self.nx
        self.rows, self.block = rows, block
        self.lanes = -(-(block + 1) // LANES) * LANES
        self.slot = self.lanes // self.ny
        self.batch = rows * dp
        right = self.ny // 2
        self.routes = []
        for step, reach in ((1, right), (-1, self.ny - 1 - right)):
            for near in range(1, reach + 1, 2):
                self.routes.append((step, near, near < reach))


class Copies:
    def __init__(self):
        self.count = 0

    def take(self, n=1):
        first = self.count
        self.count += n
        return first


def build(p):
    copies = Copies()
    nx, ny, nh, nz, nc, nq = p.nx, p.ny, p.nh, p.nz, p.nc, p.nq
    rows, lanes, slot, block = p.rows, p.lanes, p.slot, p.block
    half = rows // nc
    quarter = half // 2
    part = rows // SUB
    routes = p.routes
    pairs_x = nx // nc
    marks = dict(
        a=copies.take(nx),
        b=copies.take(nx * nq),
        pass_z=copies.take(nx * nq),
        pass_c=copies.take(nx * nq),
        stat_x=copies.take(nx),
        stat_y=copies.take(ny),
        stat_h=copies.take(nh),
        mid=copies.take(len(routes) * nq),
        fin=copies.take(len(routes) * nq),
        swap=copies.take(nq),
        near=copies.take(len(routes) * nq),
        far=copies.take(len(routes) * nq),
        pair=copies.take(pairs_x * nq),
        back_a=copies.take(nx),
        scatter=copies.take(max(pairs_x, nx) * nq),
        chain=copies.take(3 * nz * SUB),
    )

    def kernel(
        za,
        zb,
        out_a,
        out_b,
        raw_a,
        raw_b,
        pack,
        low_a,
        low_b,
        low_t,
        stat_x,
        stat_y,
        stat_h,
        mean,
        tile,
        mid_in,
        mid_out,
        fin_in,
        owned,
        swap_out,
        swap_in,
        grad,
        acc_a,
        send_a,
        recv_a,
        blocks,
        pair,
        scatter_out,
        line,
        chain_in,
        chain_out,
        owned_b,
        send_sem,
        recv_sem,
        own_sem,
    ):
        dp = lax.axis_index("dp")
        fs = lax.axis_index("fsdp")
        x = dp % nx
        h = (dp // nx) % nh
        y = dp // (nx * nh)
        core = fs % nc
        zl = fs // nc

        def device(x=x, y=y, h=h, zl=zl, core=core):
            return {"dp": (y * nh + h) * nx + x, "fsdp": zl * nc + core}

        def remote(src, dst, mark, there, recv_mark=None):
            arrived = mark if recv_mark is None else recv_mark
            return pltpu.make_async_remote_copy(
                src_ref=src,
                dst_ref=dst,
                send_sem=send_sem.at[mark],
                recv_sem=recv_sem.at[arrived],
                device_id=there,
                device_id_type=MESH,
            )

        barrier = pltpu.get_barrier_semaphore()

        def greet(there):
            pl.semaphore_signal(barrier, inc=1, device_id=there, device_id_type=MESH)

        greet(device(core=1 - core))
        for k in range(1, nx):
            greet(device(x=(x + k) % nx))
            greet(device(x=(x + k) % nx, core=1 - core))
        for k in range(1, ny):
            greet(device(y=(y + k) % ny))
        greet(device(h=1 - h))
        for k in range(1, nz):
            greet(device(zl=(zl + k) % nz))

        waiting = []

        zero = jnp.zeros((rows, lanes - block), BF16)
        raw_a[x] = jnp.concatenate([za[...], zero], axis=1)
        for f in range(p.nf):
            piece = zb[:, f * block : (f + 1) * block]
            pack[f // nq, f % nq] = jnp.concatenate([piece, zero], axis=1)

        def sums(value):
            v = value.astype(F32)
            return (
                jnp.sum(v, axis=0, keepdims=True),
                jnp.sum(v * v, axis=0, keepdims=True),
            )

        first = [sums(pack[f // nq, f % nq]) for f in range(p.nf)]
        first_a = sums(raw_a[x])
        for t in range(nx):
            both = first[t * nq : (t + 1) * nq] + [first_a]
            stat_x[0, t] = jnp.concatenate(
                [s for s, _ in both] + [s for _, s in both], axis=0
            )

        pl.semaphore_wait(barrier, 2 * (nx - 1) + ny - 1 + nz - 1 + 2)

        def start(copy):
            copy.start()
            waiting.append(copy)
            return copy

        got_x, got_y = {}, {}
        for k in range(1, nx):
            t = (x + k) % nx
            got_x[k] = start(
                remote(
                    stat_x.at[0, t],
                    stat_x.at[1, k],
                    marks["stat_x"] + k,
                    device(x=t),
                )
            )
        into_a = {}
        for k in range(1, nx):
            into_a[k] = start(
                remote(
                    raw_a.at[x], raw_a.at[x], marks["a"] + k, device(x=(x + k) % nx)
                )
            )
        own_rows = pl.ds(core * half + (zl % 2) * quarter, quarter)
        core_rows = pl.ds(core * half, half)
        z_pair = device(zl=zl + 1 - 2 * (zl % 2))
        into_b = {}
        for q in range(nq):
            for k in range(1, nx):
                t = (x + k) % nx
                into_b[q, k] = start(
                    remote(
                        pack.at[t, q, own_rows],
                        raw_b.at[q, x, own_rows],
                        marks["b"] + q * nx + k,
                        device(x=t),
                    )
                )
        mine = []
        for q in range(nq):
            copy = pltpu.make_async_copy(pack.at[x, q], raw_b.at[q, x], own_sem.at[q])
            copy.start()
            mine.append(copy)

        total = stat_x[0, x]
        for k in range(1, nx):
            got_x[k].wait_recv()
            total = total + stat_x[1, k]
        stat_y[0] = total
        for k in range(1, ny):
            got_y[k] = start(
                remote(
                    stat_y.at[0],
                    stat_y.at[k],
                    marks["stat_y"] + k,
                    device(y=(y + k) % ny),
                )
            )
        for k in range(1, ny):
            got_y[k].wait_recv()
            total = total + stat_y[k]
        stat_h[0] = total
        other = start(
            remote(stat_h.at[0], stat_h.at[1], marks["stat_h"], device(h=1 - h))
        )
        other.wait_recv()
        total = (total + stat_h[1]) / p.batch
        count = nq + 1
        center = total[:count]
        inverse = lax.rsqrt(total[count:] - center * center + EPS)
        mean[:count] = center
        mean[count:] = inverse

        lane = lax.broadcasted_iota(jnp.int32, (rows, lanes), 1)

        def normal(raw, which):
            v = raw.astype(F32)
            return (v - mean[which : which + 1, :]) * mean[
                count + which : count + which + 1, :
            ]

        def low(raw, which):
            return jnp.where(lane == block, 1.0, normal(raw, which)).astype(BF16)

        for k in range(1, nx):
            into_a[k].wait_recv()

        def low_a_step(i, _):
            low_a[i] = low(raw_a[i], nq)
            return 0

        lax.fori_loop(0, nx, low_a_step, 0)
        for i in range(nx):
            low_t[:, i * rows : (i + 1) * rows] = jnp.transpose(
                low_a[i].astype(F32)
            ).astype(BF16)

        passed_z, passed, swaps, pairs = {}, {}, {}, {}
        mid, fin, near_ag, far_ag = {}, {}, {}, {}

        def pass_z(q):
            for k in range(1, nx):
                into_b[q, k].wait_recv()
                s = (x + nx - k) % nx
                passed_z[q, k] = start(
                    remote(
                        raw_b.at[q, s, own_rows],
                        raw_b.at[q, s, own_rows],
                        marks["pass_z"] + q * nx + k,
                        z_pair,
                    )
                )

        def pass_core(q):
            for k in range(1, nx):
                passed_z[q, k].wait_recv()
                s = (x + nx - k) % nx
                passed[q, k] = start(
                    remote(
                        raw_b.at[q, s, core_rows],
                        raw_b.at[q, s, core_rows],
                        marks["pass_c"] + q * nx + k,
                        device(core=1 - core),
                    )
                )

        def along(distance):
            return (y + distance + ny) % ny

        def make_tile(q):
            mine[q].wait()
            for k in range(1, nx):
                passed[q, k].wait_recv()

            def low_b_step(i, _):
                low_b[q, i] = low(raw_b[q, i], q)
                return 0

            lax.fori_loop(0, nx, low_b_step, 0)
            product = jnp.dot(
                low_t[...],
                low_b[q].reshape(nx * rows, lanes),
                preferred_element_type=F32,
            )
            tile[q] = product.astype(BF16).reshape(ny, slot, lanes)
            for r, (step, near, goes_on) in enumerate(routes):
                mark = r * nq + q
                if goes_on:
                    t = along(step * (near + 1))
                    mid[r, q] = start(
                        remote(
                            tile.at[q, t],
                            mid_in.at[r, q],
                            marks["mid"] + mark,
                            device(y=along(step)),
                        )
                    )
                else:
                    t = along(step * near)
                    fin[r, q] = start(
                        remote(
                            tile.at[q, t],
                            fin_in.at[r, q],
                            marks["fin"] + mark,
                            device(y=t),
                        )
                    )

        def sum_step(q):
            for r, (step, near, goes_on) in enumerate(routes):
                if goes_on:
                    t = along(step * near)
                    mid[r, q].wait_recv()
                    mid_out[r, q] = (
                        mid_in[r, q].astype(F32) + tile[q, t].astype(F32)
                    ).astype(BF16)
                    fin[r, q] = start(
                        remote(
                            mid_out.at[r, q],
                            fin_in.at[r, q],
                            marks["fin"] + r * nq + q,
                            device(y=t),
                        )
                    )

        def swap_step(q):
            value = tile[q, y].astype(F32)
            for r in range(len(routes)):
                fin[r, q].wait_recv()
                value = value + fin_in[r, q].astype(F32)
            owned[q] = value
            swap_out[q] = value.astype(BF16)
            swaps[q] = start(
                remote(
                    swap_out.at[q], swap_in.at[q], marks["swap"] + q, device(h=1 - h)
                )
            )

        def grad_step(q):
            swaps[q].wait_recv()
            corr = (owned[q] + swap_in[q].astype(F32)) / p.batch
            row = y * slot + lax.broadcasted_iota(jnp.int32, (slot, lanes), 0)
            col = lax.broadcasted_iota(jnp.int32, (slot, lanes), 1)
            on = (row == col) & (fs == nq * x + q)
            grad[q, y] = jnp.where(
                on, -2.0 * (1.0 - corr), 2.0 * WEIGHT * corr
            ).astype(BF16)
            for r, (step, near, goes_on) in enumerate(routes):
                near_ag[r, q] = start(
                    remote(
                        grad.at[q, y],
                        grad.at[q, y],
                        marks["near"] + r * nq + q,
                        device(y=along(step * near)),
                    )
                )

        def gather_step(q):
            for r, (step, near, goes_on) in enumerate(routes):
                near_ag[r, q].wait_recv()
                if goes_on:
                    t = along(-step * near)
                    far_ag[r, q] = start(
                        remote(
                            grad.at[q, t],
                            grad.at[q, t],
                            marks["far"] + r * nq + q,
                            device(y=along(step)),
                        )
                    )

        means_a = [jnp.zeros((1, lanes), F32), jnp.zeros((1, lanes), F32)]

        def back_step(q):
            for r, (step, near, goes_on) in enumerate(routes):
                if goes_on:
                    far_ag[r, q].wait_recv()
            row = lax.broadcasted_iota(jnp.int32, (lanes, lanes), 0)
            col = lax.broadcasted_iota(jnp.int32, (lanes, lanes), 1)
            g = grad[q].reshape(lanes, lanes).astype(F32)
            mean_b = g[block : block + 1, :] / (2.0 * WEIGHT)
            mean_a = g[:, block : block + 1] / (2.0 * WEIGHT)
            g = jnp.where((row < block) & (col < block), g, 0.0)
            on = (row == col) & (fs == nq * x + q)
            cross = g * jnp.where(on, 1.0 + 0.5 * g, g / (2.0 * WEIGHT))
            flat_b = jnp.sum(g * mean_a, axis=0, keepdims=True)
            cross_b = jnp.sum(cross, axis=0, keepdims=True)
            low_g = g.astype(BF16)

            def back_b_step(i, _):
                value = jnp.dot(low_a[i], low_g, preferred_element_type=F32)
                value = value - flat_b - normal(raw_b[q, i], q) * cross_b
                blocks[i, q] = (value * mean[count + q : count + q + 1, :]).astype(BF16)
                return 0

            lax.fori_loop(0, nx, back_b_step, 0)
            for m in range(nx // nc):
                pairs[m, q] = start(
                    remote(
                        blocks.at[m * nc + 1 - core, q],
                        pair.at[m, q],
                        marks["pair"] + m * nq + q,
                        device(core=1 - core),
                    )
                )

            means_a[0] += jnp.sum(jnp.transpose(g * mean_b), axis=0, keepdims=True)
            means_a[1] += jnp.sum(jnp.transpose(cross), axis=0, keepdims=True)

            def back_a_step(i, _):
                value = lax.dot_general(
                    low_b[q, i],
                    low_g,
                    (((1,), (1,)), ((), ())),
                    preferred_element_type=F32,
                )
                acc_a[i] = value if q == 0 else acc_a[i] + value
                return 0

            lax.fori_loop(0, nx, back_a_step, 0)

        backs = {}

        def close_a():
            inv_a = mean[count + nq : count + nq + 1, :]

            def close_a_step(i, _):
                value = acc_a[i] - means_a[0] - normal(raw_a[i], nq) * means_a[1]
                value = value * inv_a
                acc_a[i] = value
                send_a[i] = value.astype(BF16)
                return 0

            lax.fori_loop(0, nx, close_a_step, 0)
            for k in range(1, nx):
                t = (x + k) % nx
                backs[k] = start(
                    remote(
                        send_a.at[t], recv_a.at[k], marks["back_a"] + k, device(x=t)
                    )
                )

        mine_f = [nq * x + q for q in range(nq)]

        def scatter_copy(m, q):
            return remote(
                scatter_out.at[m, q],
                line.at[mine_f[q] // nc],
                marks["scatter"] + q * pairs_x + m,
                device(x=m * nc + core, core=mine_f[q] % nc),
                marks["scatter"] + q * nx + x,
            )

        def stays(m, q):
            return (m * nc + core == x) & (mine_f[q] % nc == core)

        def scatter_step(q):
            for m in range(pairs_x):
                pairs[m, q].wait_recv()
                value = blocks[m * nc + core, q].astype(F32) + pair[m, q].astype(F32)
                value = value.astype(BF16).reshape(SUB, part, lanes)

                @pl.when(stays(m, q))
                def _():
                    line[mine_f[q] // nc] = value

                @pl.when(jnp.logical_not(stays(m, q)))
                def _():
                    scatter_out[m, q] = value
                    scatter_copy(m, q).start()

        middle = nz // 2
        low_half = zl < middle

        def chain_copy(kind, d, s, there):
            return remote(
                chain_out.at[d, s],
                chain_in.at[kind, d, s],
                marks["chain"] + d * SUB + s,
                device(zl=there),
                marks["chain"] + (kind * nz + d) * SUB + s,
            )

        def chain_place(d):
            same = low_half if d < middle else jnp.logical_not(low_half)
            first, end = (0, middle - 1) if d < middle else (middle, nz - 1)
            up = zl < d
            kind = jnp.where(same, jnp.where(up, 0, 1), 2)
            edge = jnp.where(low_half, middle - 1, middle)
            beside = jnp.where(up, zl + 1, zl - 1)
            there = jnp.where(jnp.logical_not(same) & (zl == edge), d, beside)
            starts = jnp.where(
                same,
                jnp.where(up, zl == first, zl == end),
                jnp.where(low_half, zl == 0, zl == nz - 1),
            )
            return kind, there, starts

        def chain_step(q, s_x):
            f = nq * s_x + q
            d = f // nc
            kind, there, starts = chain_place(d)

            @pl.when(core == f % nc)
            def _():
                @pl.when(jnp.logical_not((x == s_x) & (core == x % nc)))
                def _():
                    remote(
                        scatter_out.at[0, q],
                        line.at[d],
                        marks["scatter"],
                        device(core=1 - core),
                        marks["scatter"] + q * nx + s_x,
                    ).wait_recv()

                @pl.when(zl != d)
                def _():
                    for s in range(SUB):

                        @pl.when(starts)
                        def _():
                            chain_out[d, s] = line[d, s]

                        @pl.when(jnp.logical_not(starts))
                        def _():
                            chain_copy(kind, d, s, there).wait_recv()
                            chain_out[d, s] = (
                                line[d, s].astype(F32)
                                + chain_in[kind, d, s].astype(F32)
                            ).astype(BF16)

                        chain_copy(kind, d, s, there).start()

        tasks = []

        def at(time, what, *which):
            tasks.append((time, len(tasks), what, which))

        gap = 3.7
        for q in range(nq):
            now = q * gap
            at(now, pass_z, q)
            at(now + 2.0, pass_core, q)
            at(now + 4.0, make_tile, q)
            at(now + 9.0, sum_step, q)
            at(now + 13.0, swap_step, q)
            at(now + 20.5, grad_step, q)
            at(now + 24.5, gather_step, q)
            at(now + 28.5, back_step, q)
            now += 28.5 + (4.0 if q < nq - 1 else 2.0)
            at(now, scatter_step, q)
            if q == nq - 1:
                at(now, close_a)
            for s_x in range(nx):
                at(now + 5.0, chain_step, q, s_x)
        for _, _, what, which in sorted(tasks, key=lambda task: task[:2]):
            what(*which)

        total_a = acc_a[x]
        for k in range(1, nx):
            backs[k].wait_recv()
            total_a = total_a + recv_a[k].astype(F32)
        out_a[...] = total_a.astype(BF16)

        here = jnp.where(low_half, zl, zl - middle)
        beside_me = (zl + 1) % nz
        for s in range(SUB):
            owned_b[...] = line[zl, s].astype(F32)
            chain_copy(2, zl, s, beside_me).wait_recv()
            owned_b[...] += chain_in[2, zl, s].astype(F32)

            @pl.when(here > 0)
            def _():
                chain_copy(0, zl, s, beside_me).wait_recv()
                owned_b[...] += chain_in[0, zl, s].astype(F32)

            @pl.when(here < middle - 1)
            def _():
                chain_copy(1, zl, s, beside_me).wait_recv()
                owned_b[...] += chain_in[1, zl, s].astype(F32)

            out_b[s * part : (s + 1) * part] = owned_b[...].astype(BF16)

        for q in range(nq):
            for m in range(pairs_x):

                @pl.when(jnp.logical_not(stays(m, q)))
                def _():
                    scatter_copy(m, q).wait_send()

        for d in range(nz):

            @pl.when(zl != d)
            def _():
                kind, there, _ = chain_place(d)
                for s in range(SUB):
                    chain_copy(kind, d, s, there).wait_send()

        for copy in waiting:
            copy.wait_send()

    vmem = pltpu.VMEM
    count = nq + 1
    shapes = [
        vmem((nx, rows, lanes), BF16),
        vmem((nq, nx, rows, lanes), BF16),
        vmem((nx, nq, rows, lanes), BF16),
        vmem((nx, rows, lanes), BF16),
        vmem((nq, nx, rows, lanes), BF16),
        vmem((lanes, nx * rows), BF16),
        vmem((2, nx, 2 * count, lanes), F32),
        vmem((ny, 2 * count, lanes), F32),
        vmem((2, 2 * count, lanes), F32),
        vmem((2 * count, lanes), F32),
        vmem((nq, ny, slot, lanes), BF16),
        vmem((len(routes), nq, slot, lanes), BF16),
        vmem((len(routes), nq, slot, lanes), BF16),
        vmem((len(routes), nq, slot, lanes), BF16),
        vmem((nq, slot, lanes), F32),
        vmem((nq, slot, lanes), BF16),
        vmem((nq, slot, lanes), BF16),
        vmem((nq, ny, slot, lanes), BF16),
        vmem((nx, rows, lanes), F32),
        vmem((nx, rows, lanes), BF16),
        vmem((nx, rows, lanes), BF16),
        vmem((nx, nq, rows, lanes), BF16),
        vmem((nx // nc, nq, rows, lanes), BF16),
        vmem((pairs_x, nq, SUB, part, lanes), BF16),
        vmem((nz, SUB, part, lanes), BF16),
        vmem((3, nz, SUB, part, lanes), BF16),
        vmem((nz, SUB, part, lanes), BF16),
        vmem((part, lanes), F32),
        pltpu.SemaphoreType.DMA((copies.count,)),
        pltpu.SemaphoreType.DMA((copies.count,)),
        pltpu.SemaphoreType.DMA((nq,)),
    ]
    result = jax.ShapeDtypeStruct((rows, lanes), BF16)
    return pl.pallas_call(
        kernel,
        out_shape=(result, result),
        in_specs=[pl.BlockSpec(memory_space=vmem)] * 2,
        out_specs=(pl.BlockSpec(memory_space=vmem),) * 2,
        scratch_shapes=shapes,
        compiler_params=pltpu.CompilerParams(
            collective_id=0, has_side_effects=True, vmem_limit_bytes=56 << 20
        ),
    )


def solution(mesh):
    def local(z_a, z_b):
        grad_a, grad_b = build(Plan(mesh, *z_a.shape))(z_a, z_b)
        block = z_a.shape[1]
        return grad_a[:, :block], grad_b[:, :block]

    return jax.shard_map(
        local,
        mesh=mesh,
        in_specs=(P("dp", "fsdp"), P("dp", None)),
        out_specs=(P("dp", "fsdp"), P("dp", "fsdp")),
        check_vma=False,
    )
```

time: 143 us -> 120 us (0.84)
  the two profiles are of different devices: /device:TPU:1 before, /device:TPU:92 now
where the time goes in v3:
time: 120 us
  Pallas kernels  116 us (97%)
  local copies, waits for them, and re-layouts  3.17 us (3%)
    pallas_call x1, Pallas kernels, local(): grad_a, grad_b = build(Plan(mesh, *z_a.shape))(z_a, z_b)  116 us
    unnamed x2, local copies, waits for them, and re-layouts  3.17 us

profile of v3, /device:TPU:92, one launch (start us, length us, event | category | flops | bytes accessed | tf_op | source)
XLA Modules:
  0.0 120.2 jit_solution(2394482247477932500)
XLA Ops:
  0.6 116.4 %shard_map.41 = (bf16[192,384]{1,0:T(8,128)(2,1)}, bf16[192,384]{1,0:T(8,128)(2,1)}) custom-call(bf16[192,352]{1,0:T(8,128)(2,1)} %za.1, bf16[192,4224]{1,0:T(8,128)(2,1)} %zb.1), custom_call_target="tpu_custom_call" | custom-call | tf_op jit(solution)/shard_map/pallas_call | solution.py:687
  117.0 1.6 %copy.6 = bf16[192,352]{1,0:T(8,128)(2,1)} copy(bf16[192,352]{1,0:T(8,128)(2,1)} %bitcast.3) | data formatting | bytes 270336
  118.6 1.6 %copy.7 = bf16[192,352]{1,0:T(8,128)(2,1)} copy(bf16[192,352]{1,0:T(8,128)(2,1)} %bitcast.2) | data formatting | bytes 270336

commit v4 on v3

--- a/solution.py
+++ b/solution.py
@@ -62,7 +62,9 @@
         pass_c=copies.take(nx * nq),
         stat_x=copies.take(nx),
         stat_y=copies.take(ny),
-        stat_h=copies.take(nh),
+        stat_h=copies.take(1),
+        low_y=copies.take(ny),
+        low_h=copies.take(1),
         mid=copies.take(len(routes) * nq),
         fin=copies.take(len(routes) * nq),
         swap=copies.take(nq),
@@ -77,8 +79,7 @@
     def kernel(
         za,
         zb,
-        out_a,
-        out_b,
+        out,
         raw_a,
         raw_b,
         pack,
@@ -88,7 +89,13 @@
         stat_x,
         stat_y,
         stat_h,
+        low_sum,
+        low_pair,
+        half_low,
+        group,
         mean,
+        shift_b,
+        column,
         tile,
         mid_in,
         mid_out,
@@ -231,20 +238,45 @@
                     device(y=(y + k) % ny),
                 )
             )
-        for k in range(1, ny):
-            got_y[k].wait_recv()
-            total = total + stat_y[k]
-        stat_h[0] = total
-        other = start(
-            remote(stat_h.at[0], stat_h.at[1], marks["stat_h"], device(h=1 - h))
-        )
-        other.wait_recv()
-        total = (total + stat_h[1]) / p.batch
         count = nq + 1
-        center = total[:count]
-        inverse = lax.rsqrt(total[count:] - center * center + EPS)
-        mean[:count] = center
-        mean[count:] = inverse
+        images = nx * rows
+        group[:count] = total[:count] / images
+        low_pair[0] = jnp.zeros((8, lanes), F32)
+        got_h, got_low = {}, {}
+
+        def half_moments():
+            total = stat_y[0]
+            for k in range(1, ny):
+                got_y[k].wait_recv()
+                total = total + stat_y[k]
+            stat_h[0] = total
+            got_h[0] = start(
+                remote(stat_h.at[0], stat_h.at[1], marks["stat_h"], device(h=1 - h))
+            )
+
+        def all_moments():
+            got_h[0].wait_recv()
+            ours, theirs = stat_h[0], stat_h[1]
+            total = (ours + theirs) / p.batch
+            center = total[:count]
+            inverse = lax.rsqrt(total[count:] - center * center + EPS)
+            mean[:count] = center
+            mean[count:] = inverse
+            half_mean = ours[:count] / (images * ny)
+            apart = half_mean - theirs[:count] / (images * ny)
+            shifts = [stat_y[k][:count] / images - half_mean for k in range(ny)]
+            fill = [jnp.zeros((16 - ny - 2, lanes), F32)] if ny < 14 else []
+            for q in range(count):
+                table = jnp.concatenate(
+                    [v[q : q + 1] for v in shifts]
+                    + [apart[q : q + 1], inverse[q : q + 1]]
+                    + fill,
+                    axis=0,
+                )
+                if q < nq:
+                    shift_b[q] = table
+                else:
+                    column[...] = jnp.transpose(table)
 
         lane = lax.broadcasted_iota(jnp.int32, (rows, lanes), 1)
 
@@ -254,21 +286,61 @@
                 count + which : count + which + 1, :
             ]
 
-        def low(raw, which):
-            return jnp.where(lane == block, 1.0, normal(raw, which)).astype(BF16)
-
-        for k in range(1, nx):
-            into_a[k].wait_recv()
-
-        def low_a_step(i, _):
-            low_a[i] = low(raw_a[i], nq)
-            return 0
-
-        lax.fori_loop(0, nx, low_a_step, 0)
-        for i in range(nx):
-            low_t[:, i * rows : (i + 1) * rows] = jnp.transpose(
-                low_a[i].astype(F32)
-            ).astype(BF16)
+        def centred(raw, which):
+            return raw.astype(F32) - group[which : which + 1, :]
+
+        def center_a():
+            for k in range(1, nx):
+                into_a[k].wait_recv()
+            for i in range(nx):
+                low_t[:, i * rows : (i + 1) * rows] = jnp.transpose(
+                    centred(raw_a[i], nq)
+                ).astype(BF16)
+
+        def normalise(which):
+            def low_step(i, _):
+                if which < nq:
+                    value = normal(raw_b[which, i], which).astype(BF16)
+                    low_b[which, i] = value
+                else:
+                    value = normal(raw_a[i], which).astype(BF16)
+                    low_a[i] = value
+                low_pair[0, which : which + 1] += jnp.sum(
+                    value.astype(F32), axis=0, keepdims=True
+                )
+                return 0
+
+            lax.fori_loop(0, nx, low_step, 0)
+
+        def low_over_y():
+            low_sum[0] = low_pair[0]
+            for k in range(1, ny):
+                got_low[k] = start(
+                    remote(
+                        low_sum.at[0],
+                        low_sum.at[k],
+                        marks["low_y"] + k,
+                        device(y=(y + k) % ny),
+                    )
+                )
+
+        def low_over_h():
+            total = low_sum[0]
+            for k in range(1, ny):
+                got_low[k].wait_recv()
+                total = total + low_sum[k]
+            half_low[...] = total
+            got_low[0] = start(
+                remote(half_low, low_pair.at[1], marks["low_h"], device(h=1 - h))
+            )
+
+        low_mean = {}
+
+        def low_means():
+            got_low[0].wait_recv()
+            value = (half_low[...] + low_pair[1]) / p.batch
+            low_mean["row"] = value
+            low_mean["column"] = jnp.transpose(value)[:, nq : nq + 1]
 
         passed_z, passed, swaps, pairs = {}, {}, {}, {}
         mid, fin, near_ag, far_ag = {}, {}, {}, {}
@@ -299,8 +371,10 @@
                     )
                 )
 
+        flip = 1 - 2 * (core % 2)
+
         def along(distance):
-            return (y + distance + ny) % ny
+            return (y + flip * distance + ny) % ny
 
         def make_tile(q):
             mine[q].wait()
@@ -308,7 +382,7 @@
                 passed[q, k].wait_recv()
 
             def low_b_step(i, _):
-                low_b[q, i] = low(raw_b[q, i], q)
+                low_b[q, i] = centred(raw_b[q, i], q).astype(BF16)
                 return 0
 
             lax.fori_loop(0, nx, low_b_step, 0)
@@ -358,11 +432,17 @@
                         )
                     )
 
+        own_slot = pl.ds(pl.multiple_of(y * slot, 8), slot)
+
         def swap_step(q):
             value = tile[q, y].astype(F32)
             for r in range(len(routes)):
                 fin[r, q].wait_recv()
                 value = value + fin_in[r, q].astype(F32)
+            spread = jnp.zeros((slot, lanes), F32)
+            for k in range(ny):
+                spread += column[own_slot, k : k + 1] * shift_b[q, k : k + 1]
+            value = value + images * spread
             owned[q] = value
             swap_out[q] = value.astype(BF16)
             swaps[q] = start(
@@ -373,7 +453,10 @@
 
         def grad_step(q):
             swaps[q].wait_recv()
-            corr = (owned[q] + swap_in[q].astype(F32)) / p.batch
+            spread = column[own_slot, ny : ny + 1] * shift_b[q, ny : ny + 1]
+            corr = owned[q] + swap_in[q].astype(F32) + (p.batch / 4) * spread
+            scale = column[own_slot, ny + 1 : ny + 2] * shift_b[q, ny + 1 : ny + 2]
+            corr = corr * scale / p.batch
             row = y * slot + lax.broadcasted_iota(jnp.int32, (slot, lanes), 0)
             col = lax.broadcasted_iota(jnp.int32, (slot, lanes), 1)
             on = (row == col) & (fs == nq * x + q)
@@ -413,8 +496,8 @@
             row = lax.broadcasted_iota(jnp.int32, (lanes, lanes), 0)
             col = lax.broadcasted_iota(jnp.int32, (lanes, lanes), 1)
             g = grad[q].reshape(lanes, lanes).astype(F32)
-            mean_b = g[block : block + 1, :] / (2.0 * WEIGHT)
-            mean_a = g[:, block : block + 1] / (2.0 * WEIGHT)
+            mean_b = low_mean["row"][q : q + 1]
+            mean_a = low_mean["column"]
             g = jnp.where((row < block) & (col < block), g, 0.0)
             on = (row == col) & (fs == nq * x + q)
             cross = g * jnp.where(on, 1.0 + 0.5 * g, g / (2.0 * WEIGHT))
@@ -524,21 +607,24 @@
             edge = jnp.where(low_half, middle - 1, middle)
             beside = jnp.where(up, zl + 1, zl - 1)
             there = jnp.where(jnp.logical_not(same) & (zl == edge), d, beside)
-            starts = jnp.where(
+            level = jnp.where(
                 same,
-                jnp.where(up, zl == first, zl == end),
-                jnp.where(low_half, zl == 0, zl == nz - 1),
-            )
-            return kind, there, starts
-
-        def chain_step(q, s_x):
+                jnp.where(up, zl - first, end - zl),
+                jnp.where(low_half, zl, nz - 1 - zl),
+            )
+            return kind, there, level
+
+        def chain_step(q, s_x, at_level):
             f = nq * s_x + q
             d = f // nc
-            kind, there, starts = chain_place(d)
-
-            @pl.when(core == f % nc)
-            def _():
-                @pl.when(jnp.logical_not((x == s_x) & (core == x % nc)))
+            kind, there, level = chain_place(d)
+
+            if at_level == 0:
+
+                @pl.when(
+                    (core == f % nc)
+                    & jnp.logical_not((x == s_x) & (core == x % nc))
+                )
                 def _():
                     remote(
                         scatter_out.at[0, q],
@@ -548,46 +634,49 @@
                         marks["scatter"] + q * nx + s_x,
                     ).wait_recv()
 
-                @pl.when(zl != d)
-                def _():
-                    for s in range(SUB):
-
-                        @pl.when(starts)
-                        def _():
-                            chain_out[d, s] = line[d, s]
-
-                        @pl.when(jnp.logical_not(starts))
-                        def _():
-                            chain_copy(kind, d, s, there).wait_recv()
-                            chain_out[d, s] = (
-                                line[d, s].astype(F32)
-                                + chain_in[kind, d, s].astype(F32)
-                            ).astype(BF16)
-
-                        chain_copy(kind, d, s, there).start()
+            @pl.when((core == f % nc) & (zl != d) & (level == at_level))
+            def _():
+                for s in range(SUB):
+                    if at_level == 0:
+                        chain_out[d, s] = line[d, s]
+                    else:
+                        chain_copy(kind, d, s, there).wait_recv()
+                        chain_out[d, s] = (
+                            line[d, s].astype(F32) + chain_in[kind, d, s].astype(F32)
+                        ).astype(BF16)
+                    chain_copy(kind, d, s, there).start()
 
         tasks = []
 
         def at(time, what, *which):
             tasks.append((time, len(tasks), what, which))
 
-        gap = 3.7
+        at(7.5, center_a)
+        at(12.6, half_moments)
+        at(20.2, all_moments)
+        at(22.8, normalise, nq)
+        at(27.5, low_over_y)
+        at(35.5, low_over_h)
+        at(43.5, low_means)
         for q in range(nq):
-            now = q * gap
-            at(now, pass_z, q)
-            at(now + 2.0, pass_core, q)
-            at(now + 4.0, make_tile, q)
-            at(now + 9.0, sum_step, q)
-            at(now + 13.0, swap_step, q)
-            at(now + 20.5, grad_step, q)
-            at(now + 24.5, gather_step, q)
-            at(now + 28.5, back_step, q)
-            now += 28.5 + (4.0 if q < nq - 1 else 2.0)
+            at(11.0 + 2.3 * q, pass_z, q)
+            at(14.0 + 2.8 * q, pass_core, q)
+            at(16.0 + 2.8 * q, make_tile, q)
+            at(23.0 + 1.8 * q, normalise, q)
+            now = 21.0 + 3.7 * q
+            at(now, sum_step, q)
+            at(now + 5.5, swap_step, q)
+            at(now + 13.5, grad_step, q)
+            at(now + 19.0, gather_step, q)
+            now += 23.0
+            at(now, back_step, q)
+            now += 4.0 if q < nq - 1 else 2.0
             at(now, scatter_step, q)
             if q == nq - 1:
                 at(now, close_a)
-            for s_x in range(nx):
-                at(now + 5.0, chain_step, q, s_x)
+            for level in range(middle):
+                for s_x in range(nx):
+                    at(now + 4.5 + 3.0 * level, chain_step, q, s_x, level)
         for _, _, what, which in sorted(tasks, key=lambda task: task[:2]):
             what(*which)
 
@@ -595,7 +684,7 @@
         for k in range(1, nx):
             backs[k].wait_recv()
             total_a = total_a + recv_a[k].astype(F32)
-        out_a[...] = total_a.astype(BF16)
+        out[0] = total_a
 
         here = jnp.where(low_half, zl, zl - middle)
         beside_me = (zl + 1) % nz
@@ -614,7 +703,7 @@
                 chain_copy(1, zl, s, beside_me).wait_recv()
                 owned_b[...] += chain_in[1, zl, s].astype(F32)
 
-            out_b[s * part : (s + 1) * part] = owned_b[...].astype(BF16)
+            out[1, s * part : (s + 1) * part] = owned_b[...]
 
         for q in range(nq):
             for m in range(pairs_x):
@@ -646,7 +735,13 @@
         vmem((2, nx, 2 * count, lanes), F32),
         vmem((ny, 2 * count, lanes), F32),
         vmem((2, 2 * count, lanes), F32),
+        vmem((ny, 8, lanes), F32),
+        vmem((2, 8, lanes), F32),
+        vmem((8, lanes), F32),
+        vmem((8, lanes), F32),
         vmem((2 * count, lanes), F32),
+        vmem((nq, 16, lanes), F32),
+        vmem((lanes, 16), F32),
         vmem((nq, ny, slot, lanes), BF16),
         vmem((len(routes), nq, slot, lanes), BF16),
         vmem((len(routes), nq, slot, lanes), BF16),
@@ -669,12 +764,12 @@
         pltpu.SemaphoreType.DMA((copies.count,)),
         pltpu.SemaphoreType.DMA((nq,)),
     ]
-    result = jax.ShapeDtypeStruct((rows, lanes), BF16)
+    result = jax.ShapeDtypeStruct((2, rows, lanes), F32)
     return pl.pallas_call(
         kernel,
-        out_shape=(result, result),
+        out_shape=result,
         in_specs=[pl.BlockSpec(memory_space=vmem)] * 2,
-        out_specs=(pl.BlockSpec(memory_space=vmem),) * 2,
+        out_specs=pl.BlockSpec(memory_space=vmem),
         scratch_shapes=shapes,
         compiler_params=pltpu.CompilerParams(
             collective_id=0, has_side_effects=True, vmem_limit_bytes=56 << 20
@@ -684,9 +779,9 @@
 
 def solution(mesh):
     def local(z_a, z_b):
-        grad_a, grad_b = build(Plan(mesh, *z_a.shape))(z_a, z_b)
+        grads = build(Plan(mesh, *z_a.shape))(z_a, z_b)
         block = z_a.shape[1]
-        return grad_a[:, :block], grad_b[:, :block]
+        return grads[0, :, :block].astype(BF16), grads[1, :, :block].astype(BF16)
 
     return jax.shard_map(
         local,

time: 120 us -> 107 us (0.89)
  the two profiles are of different devices: /device:TPU:92 before, /device:TPU:1 now
where the time goes in v4:
time: 107 us; the launch traced here: 105 us
  Pallas kernels  103 us (96%)
  other arithmetic  1.1 us (1%)
    pallas_call x1, Pallas kernels, local(): grads = build(Plan(mesh, *z_a.shape))(z_a, z_b)  103 us

profile of v4, /device:TPU:1, one launch (start us, length us, event | category | flops | bytes accessed | tf_op | source)
XLA Modules:
  0.0 105.2 jit_solution(8502924497599327194)
XLA Ops:
  0.6 102.7 %shard_map.41 = f32[2,192,384]{2,1,0:T(8,128)} custom-call(bf16[192,352]{1,0:T(8,128)(2,1)} %za.1, bf16[192,4224]{1,0:T(8,128)(2,1)} %zb.1), custom_call_target="tpu_custom_call" | custom-call | tf_op jit(solution)/shard_map/pallas_call | solution.py:782
  103.3 1.1 %convert.4 = bf16[2,192,384]{2,1,0:T(8,128)(2,1)S(1)} convert(f32[2,192,384]{2,1,0:T(8,128)} %shard_map.41) | non-fusion elementwise | flops 147456 | bytes 884736 | tf_op jit(solution)/shard_map/convert.1
  104.4 0.7 slice_bitcast_fusion

commit v5 on v4

--- a/solution.py
+++ b/solution.py
@@ -203,7 +203,7 @@
                     raw_a.at[x], raw_a.at[x], marks["a"] + k, device(x=(x + k) % nx)
                 )
             )
-        own_rows = pl.ds(core * half + (zl % 2) * quarter, quarter)
+        own_rows = pl.ds(core * half, half)
         core_rows = pl.ds(core * half, half)
         z_pair = device(zl=zl + 1 - 2 * (zl % 2))
         into_b = {}
@@ -346,21 +346,11 @@
         mid, fin, near_ag, far_ag = {}, {}, {}, {}
 
         def pass_z(q):
+            pass
+
+        def pass_core(q):
             for k in range(1, nx):
                 into_b[q, k].wait_recv()
-                s = (x + nx - k) % nx
-                passed_z[q, k] = start(
-                    remote(
-                        raw_b.at[q, s, own_rows],
-                        raw_b.at[q, s, own_rows],
-                        marks["pass_z"] + q * nx + k,
-                        z_pair,
-                    )
-                )
-
-        def pass_core(q):
-            for k in range(1, nx):
-                passed_z[q, k].wait_recv()
                 s = (x + nx - k) % nx
                 passed[q, k] = start(
                     remote(
@@ -653,30 +643,30 @@
 
         at(7.5, center_a)
         at(12.6, half_moments)
-        at(20.2, all_moments)
-        at(22.8, normalise, nq)
-        at(27.5, low_over_y)
-        at(35.5, low_over_h)
-        at(43.5, low_means)
+        at(23.0, all_moments)
+        at(24.2, normalise, nq)
+        at(28.2, low_over_y)
+        at(34.0, low_over_h)
+        at(41.3, low_means)
         for q in range(nq):
             at(11.0 + 2.3 * q, pass_z, q)
-            at(14.0 + 2.8 * q, pass_core, q)
-            at(16.0 + 2.8 * q, make_tile, q)
-            at(23.0 + 1.8 * q, normalise, q)
-            now = 21.0 + 3.7 * q
+            at(12.0 + 3.7 * q, pass_core, q)
+            at(13.5 + 3.7 * q, make_tile, q)
+            at((24.4, 24.6, 28.0)[q] if nq == 3 else 28.0, normalise, q)
+            now = 18.5 + 3.7 * q
             at(now, sum_step, q)
             at(now + 5.5, swap_step, q)
             at(now + 13.5, grad_step, q)
             at(now + 19.0, gather_step, q)
             now += 23.0
             at(now, back_step, q)
-            now += 4.0 if q < nq - 1 else 2.0
+            now += 2.0
             at(now, scatter_step, q)
             if q == nq - 1:
                 at(now, close_a)
             for level in range(middle):
                 for s_x in range(nx):
-                    at(now + 4.5 + 3.0 * level, chain_step, q, s_x, level)
+                    at(now + 5.0 + 2.5 * level, chain_step, q, s_x, level)
         for _, _, what, which in sorted(tasks, key=lambda task: task[:2]):
             what(*which)
 
@@ -684,7 +674,7 @@
         for k in range(1, nx):
             backs[k].wait_recv()
             total_a = total_a + recv_a[k].astype(F32)
-        out[0] = total_a
+        out[0] = total_a.astype(BF16)
 
         here = jnp.where(low_half, zl, zl - middle)
         beside_me = (zl + 1) % nz
@@ -703,7 +693,7 @@
                 chain_copy(1, zl, s, beside_me).wait_recv()
                 owned_b[...] += chain_in[1, zl, s].astype(F32)
 
-            out[1, s * part : (s + 1) * part] = owned_b[...]
+            out[1, s * part : (s + 1) * part] = owned_b[...].astype(BF16)
 
         for q in range(nq):
             for m in range(pairs_x):
@@ -764,7 +754,7 @@
         pltpu.SemaphoreType.DMA((copies.count,)),
         pltpu.SemaphoreType.DMA((nq,)),
     ]
-    result = jax.ShapeDtypeStruct((2, rows, lanes), F32)
+    result = jax.ShapeDtypeStruct((2, rows, lanes), BF16)
     return pl.pallas_call(
         kernel,
         out_shape=result,
@@ -781,7 +771,7 @@
     def local(z_a, z_b):
         grads = build(Plan(mesh, *z_a.shape))(z_a, z_b)
         block = z_a.shape[1]
-        return grads[0, :, :block].astype(BF16), grads[1, :, :block].astype(BF16)
+        return grads[0, :, :block], grads[1, :, :block]
 
     return jax.shard_map(
         local,

time: 107 us -> 101 us (0.944)
  the two profiles are of different devices: /device:TPU:1 before, /device:TPU:70 now
where the time goes in v5:
time: 101 us; the launch traced here: 100 us
  Pallas kernels  98 us (97%)
  local copies, waits for them, and re-layouts  1.72 us (2%)
    pallas_call x1, Pallas kernels, local(): grads = build(Plan(mesh, *z_a.shape))(z_a, z_b)  98 us

profile of v5, /device:TPU:70, one launch (start us, length us, event | category | flops | bytes accessed | tf_op | source)
XLA Modules:
  0.0 100.3 jit_solution(14482619188630329655)
XLA Ops:
  0.6 98.0 %shard_map.41 = bf16[2,192,384]{2,1,0:T(8,128)(2,1)} custom-call(bf16[192,352]{1,0:T(8,128)(2,1)} %za.1, bf16[192,4224]{1,0:T(8,128)(2,1)} %zb.1), custom_call_target="tpu_custom_call" | custom-call | tf_op jit(solution)/shard_map/pallas_call | solution.py:772
  98.6 1.7 %slice_bitcast_fusion = (bf16[192,352]{1,0:T(8,128)(2,1)}, bf16[192,352]{1,0:T(8,128)(2,1)}) fusion(bf16[2,192,384]{2,1,0:T(8,128)(2,1)} %shard_map.41), kind=kLoop, calls=%fused_computation | loop fusion | bytes 540672 | tf_op jit(solution)/shard_map/squeeze | solution.py:774

commit v6 on v5

--- a/solution.py
+++ b/solution.py
@@ -34,6 +34,7 @@
         for step, reach in ((1, right), (-1, self.ny - 1 - right)):
             for near in range(1, reach + 1, 2):
                 self.routes.append((step, near, near < reach))
+        self.routes.sort(key=lambda route: -route[1])
 
 
 class Copies:
@@ -464,7 +465,7 @@
                 )
 
         def gather_step(q):
-            for r, (step, near, goes_on) in enumerate(routes):
+            for r, (step, near, goes_on) in reversed(list(enumerate(routes))):
                 near_ag[r, q].wait_recv()
                 if goes_on:
                     t = along(-step * near)

time: 101 us -> 101 us (level)
  the two profiles are of different devices: /device:TPU:70 before, /device:TPU:78 now
where the time goes in v6:
time: 101 us
  Pallas kernels  98.2 us (97%)
  local copies, waits for them, and re-layouts  1.72 us (2%)
    pallas_call x1, Pallas kernels, local(): grads = build(Plan(mesh, *z_a.shape))(z_a, z_b)  98.2 us

profile of v6, /device:TPU:78, one launch (start us, length us, event | category | flops | bytes accessed | tf_op | source)
XLA Modules:
  0.0 100.5 jit_solution(2309289840383579315)
XLA Ops:
  0.6 98.2 %shard_map.41 = bf16[2,192,384]{2,1,0:T(8,128)(2,1)} custom-call(bf16[192,352]{1,0:T(8,128)(2,1)} %za.1, bf16[192,4224]{1,0:T(8,128)(2,1)} %zb.1), custom_call_target="tpu_custom_call" | custom-call | tf_op jit(solution)/shard_map/pallas_call | solution.py:773
  98.8 1.7 %slice_bitcast_fusion = (bf16[192,352]{1,0:T(8,128)(2,1)}, bf16[192,352]{1,0:T(8,128)(2,1)}) fusion(bf16[2,192,384]{2,1,0:T(8,128)(2,1)} %shard_map.41), kind=kLoop, calls=%fused_computation | loop fusion | bytes 540672 | tf_op jit(solution)/shard_map/squeeze | solution.py:775
